TPU v7x, 256 devices: a whole 4x4x8 slice. The times are simulated.
256 devices in a mesh: kv: 4 (over y), seq: 64 (over z, x, core).
Axes of the slice: x: 4, y: 4, z: 8, core: 2. Of those that a mesh axis runs over, the one named last changes fastest.
Arguments:
- sampled_rows: int32 [6144], replicated, may hold values from 0 to 16383, as said below
- query_vectors: bfloat16 [6144, 64, 128], P('seq', 'kv'), may hold values from -150 to 150
- key_vectors: bfloat16 [16384, 8, 128], P('seq', 'kv'), may hold values from -6 to 6
Outputs:
- heavy_hitters: float32 [16384], P('seq')
Inputs may be any that keep to these rules, and one draw needn't show every extreme that they name: `sampled_rows`: strictly increasing sequence positions.
All inputs are finite; a program needn't handle non-finite values.
Results may differ from a plain program's by a relative error of at most 0.0003.
Values may be sent and summed in bfloat16 or wider, within the bound.
A program may use at most 64 MiB of HBM per device.

v0:
```python
import math

import jax
import jax.numpy as jnp
from jax import lax
from jax.sharding import PartitionSpec as P

HD = 128


NEG = -1e30


def split_up(array, dim, devices):
    before, after = (array.shape[:dim], array.shape[dim + 1 :])
    return jnp.moveaxis(array.reshape(*before, devices, -1, *after), dim, 0)


def sum_at_owner(array, axis, dim):
    devices = lax.axis_size(axis)
    tiles = lax.all_to_all(split_up(array, dim, devices), axis, 0, 0, tiled=True)
    return jnp.sum(tiles, axis=0)


def copy_for_each(array, axis):
    copies = jnp.broadcast_to(array, (lax.axis_size(axis), *array.shape))
    return lax.all_to_all(copies, axis, split_axis=0, concat_axis=0, tiled=True)


def of_everyone(array, axis):
    return copy_for_each(array, axis).sum(axis=0)


def block_scores(query_block, key_block, factor):
    return (
        jnp.einsum("rgid,kgd->rgik", query_block, key_block, preferred_element_type=jnp.float32)
        * factor
    )


def visibility(rows_block, offset, amount):
    places = offset + jnp.arange(amount, dtype=jnp.int32)
    return places[None, None, None, :] <= rows_block[:, None, None, None]


def stats_block(query_block, rows_block, key_block, offset, running, factor):
    row_max, row_total = running
    scores = block_scores(query_block, key_block, factor)
    visible = visibility(rows_block, offset, key_block.shape[0])
    scores = jnp.where(visible, scores, NEG)
    new_max = jnp.maximum(row_max, jnp.max(scores, axis=-1))
    terms = jnp.where(visible, jnp.exp(scores - new_max[..., None]), 0.0)
    return (new_max, row_total * jnp.exp(row_max - new_max) + jnp.sum(terms, axis=-1))


def prob_columns(query_block, rows_block, key_block, offset, log_total, factor):
    scores = block_scores(query_block, key_block, factor)
    visible = visibility(rows_block, offset, key_block.shape[0])
    probability = jnp.where(visible, jnp.exp(scores - log_total[..., None]), 0.0)
    return jnp.sum(probability, axis=(0, 1, 2))


def on_device(sampled_rows, query_vectors, key_vectors):
    local_rows = query_vectors.shape[0]
    local_keys = key_vectors.shape[0]
    local_groups = key_vectors.shape[1]
    group_size = query_vectors.shape[1] // local_groups
    factor = 1.0 / math.sqrt(HD)
    seq_index = lax.axis_index("seq")
    grouped = query_vectors.reshape(local_rows, local_groups, group_size, HD)
    own_rows = lax.dynamic_slice_in_dim(sampled_rows, seq_index * local_rows, local_rows, 0)
    highest = jnp.max(own_rows)
    gathered = lax.all_gather(key_vectors, "seq", axis=0, tiled=True)
    total_keys = gathered.shape[0]
    key_stride = math.gcd(total_keys, 2048)

    def sweep(running, key_index):
        offset = key_index * key_stride

        def sweep_active(state):
            key_block = lax.dynamic_slice_in_dim(gathered, offset, key_stride, 0)
            return stats_block(grouped, own_rows, key_block, offset, state, factor)

        return (lax.cond(offset <= highest, sweep_active, lambda state: state, running), None)

    initial = (
        jnp.full((local_rows, local_groups, group_size), NEG, jnp.float32),
        jnp.zeros((local_rows, local_groups, group_size), jnp.float32),
    )
    (row_max, row_total), _ = lax.scan(
        sweep, initial, jnp.arange(total_keys // key_stride, dtype=jnp.int32)
    )
    log_total = row_max + jnp.log(row_total)

    def terms(offset, amount):
        stride = math.gcd(amount, 2048)

        def portion(block_index):
            first = block_index * stride

            def portion_active():
                key_block = lax.dynamic_slice_in_dim(gathered, first, stride, 0)
                return prob_columns(grouped, own_rows, key_block, first, log_total, factor)

            return lax.cond(
                first <= highest, portion_active, lambda: jnp.zeros((stride,), jnp.float32)
            )

        return lax.map(portion, jnp.arange(amount // stride, dtype=jnp.int32)).reshape(amount)

    columns = sum_at_owner(terms(jnp.int32(0), local_keys * lax.axis_size("seq")), "seq", 0)
    summed = of_everyone(columns, "kv")
    return summed * (1.0 / group_size)


def solution(mesh):
    placed = (P(), P("seq", "kv", None), P("seq", "kv", None))
    return jax.shard_map(on_device, mesh=mesh, in_specs=placed, out_specs=P("seq"), check_vma=False)
```

profile of v0, /device:TPU:1, one launch (start us, length us, event | category | flops | bytes accessed | tf_op | source)
XLA Modules:
  0.0 263.4 jit_solution(13679895400350161696)
XLA Ops:
  6.5 0.0 all-gather.2.cloned.1.call-start
  6.5 1.6 copy.10
  8.1 0.0 all-gather.2.cloned.1.call-update
  8.2 1.1 copy.11
  9.3 1.5 fusion.11
  10.7 86.6 %all-gather.2.cloned.1.call-done = bf16[16384,2,128]{2,0,1:T(8,128)(2,1)} async-done(((bf16[256,2,128]{2,0,1:T(8,128)(2,1)}), bf16[16384,2,128]{2,0,1:T(8,128)(2,1)}) %all-gather.2.cloned.1.call-update) | async-done | bytes 8388624 | tf_op jit(solution)/shard_map/all_gather | solution.py:73
  97.4 22.9 %while.22 = (s32[]{:T(128)}, f32[96,2,8]{0,2,1:T(8,128)S(1)}, f32[96,2,8]{0,2,1:T(8,128)S(1)}, s32[8]{0:T(128)S(1)}, s32[]{:T(128)}, /*index=5*/s32[96]{0:T(128)...) while((s32[]{:T(128)}, f32[96,2,8]{0,2,1:T(8,128)S(1)}, ...), condition=%wide.region_6.7_spmd, body=%wide.region_1.6_spmd.sunk | while | flops 830673920 | bytes 27294348 | solution.py:90
  97.4 0.6 dynamic_slice.30
  99.3 7.4 %conditional.4 = ((f32[96,2,8]{0,2,1:T(8,128)S(1)}, f32[96,2,8]{0,2,1:T(8,128)S(1)})) conditional(s32[]{:T(128)} %convert_element_type.8, (f32[96,2,8]{0,2,1:T(8,128)S(1)}, f32[96,2,8]{0,2,1:T(8,128)S(1)}) %tuple.51, (s32[]{:T(128)}, s32[96]{0:T(128)S(1)}, bf16[16384,2,128]{2,0,1:T(8,128)(2,1)}, bf16[96,2,8,128]{3,0,2,1:T(8,128)(2,1)S(1)}, ...), branch_computations={%region_2.2_spmd, %region_3.5_spmd} | conditional | flops 830673920 | bytes 27294146 | solution.py:84
  99.3 0.2 broadcast_compare_fusion
  99.5 3.7 %fusion = (f32[96,2,8]{0,2,1:T(8,128)S(1)}, f32[2,2048,96,8]{1,2,3,0:T(8,128)S(1)}) fusion(pred[96,2048]{1,0:T(8,128)(4,1)S(1)} %broadcast_compare_fusion, bf16[96,2,8,128]{3,0,2,1:T(8,128)(2,1)S(1)} %get-tuple-element.103, bf16[16384,2,128]{2,0,1:T(8,128)(2,1)} %get-tuple-element.102, s32[]{:T(128)S(6)} %select_n.13), kind=kOutput, calls=%fused_computation.2 | convolution fusion | flops 814742016 | bytes 14227460 | tf_op jit(solution)/shard_map/while/body/eval_jaxpr/cond/branch_1_fun/rgid,kgd->rgik/dot_general | solution.py:36
  103.1 3.5 %select_reduce_fusion = f32[96,2,8]{0,2,1:T(8,128)S(1)} fusion(f32[2,2048,96,8]{1,2,3,0:T(8,128)S(1)} %get-tuple-element.171, f32[96,2,8]{0,2,1:T(8,128)S(1)} %max.2, pred[96,2048]{1,0:T(8,128)(4,1)S(1)} %broadcast_compare_fusion), kind=kLoop, calls=%fused_computation.1 | loop fusion | flops 15727104 | bytes 12791808 | tf_op jit(solution)/shard_map/while/body/eval_jaxpr/cond/branch_1_fun/reduce_sum | solution.py:53
  106.7 0.6 dynamic_slice.30
  108.7 0.6 dynamic_slice.30
  110.6 0.6 dynamic_slice.30
  112.5 0.6 dynamic_slice.30
  114.5 0.6 dynamic_slice.30
  116.4 0.6 dynamic_slice.30
  118.4 0.6 dynamic_slice.30
  120.3 22.7 %while.23 = (s32[]{:T(128)}, f32[8,2048]{1,0:T(8,128)S(1)}, s32[8]{0:T(128)S(1)}, s32[]{:T(128)}, s32[96]{0:T(128)S(1)}, /*index=5*/bf16[16384,2,128]{2,0,1:T(8,...) while((s32[]{:T(128)}, f32[8,2048]{1,0:T(8,128)S(1)}, ...), condition=%wide.region_11.12_spmd, body=%wide.region_7.11_spmd.sunk | while | flops 818085888 | bytes 1882737 | solution.py:109
  120.3 0.6 dynamic_slice.31
  122.2 5.4 %conditional.5 = (f32[1,2048]{1,0:T(1,128)S(1)}) conditional(s32[]{:T(128)} %convert_element_type.9, () %tuple.54, (s32[]{:T(128)}, s32[96]{0:T(128)S(1)}, bf16[16384,2,128]{2,0,1:T(8,128)(2,1)}, bf16[96,2,8,128]{3,0,2,1:T(8,128)(2,1)S(1)}, f32[96,2,8]{0,2,1:T(8,128)S(1)}) %tuple.55), branch_computations={%region_8.8_spmd, %region_9.10_spmd} | conditional | flops 818085888 | bytes 1866162 | solution.py:105
  122.3 0.2 broadcast_compare_fusion.1
  122.5 5.1 %fusion.7 = f32[2048]{0:T(1024)S(1)} fusion(f32[96,2,8]{0,2,1:T(8,128)S(1)} %get-tuple-element.120, pred[96,2048]{1,0:T(8,128)(4,1)S(1)} %broadcast_compare_fusion.1, bf16[96,2,8,128]{3,0,2,1:T(8,128)(2,1)S(1)} %get-tuple-element.119, bf16[16384,2,128]{2,0,1:T(8,128)(2,1)} %get-tuple-element.118, s32[]{:T(128)S(6)} %select_n.16), kind=kOutput, calls=%fused_computation.13 | convolution fusion | flops 817887232 | bytes 1652740 | tf_op jit(solution)/shard_map/while/body/eval_jaxpr/cond/branch_1_fun/rgid,kgd->rgik/dot_general | solution.py:36
  127.6 0.2 dynamic_update_slice.5
  127.8 0.6 dynamic_slice.31
  129.8 0.2 dynamic_update_slice.5
  130.0 0.6 dynamic_slice.31
  131.9 0.2 dynamic_update_slice.5
  132.2 0.6 dynamic_slice.31
  134.1 0.2 dynamic_update_slice.5
  134.3 0.6 dynamic_slice.31
  136.3 0.2 dynamic_update_slice.5
  136.5 0.6 dynamic_slice.31
  138.4 0.2 dynamic_update_slice.5
  138.7 0.6 dynamic_slice.31
  140.6 0.2 dynamic_update_slice.5
  140.8 0.6 dynamic_slice.31
  142.8 0.2 dynamic_update_slice.5
  143.0 0.1 all_to_all.10
  143.1 104.8 %all_to_all.15 = f32[64,1,256]{2,1,0:T(1,128)S(1)} all-to-all(f32[64,1,256]{2,1,0:T(1,128)S(1)} %all_to_all.10), channel_id=1, replica_groups=mesh['kv'=4,'seq'=64] {'seq'}, dimensions={0} | all-to-all | bytes 131072 | tf_op jit(solution)/shard_map/all_to_all | solution.py:21
  247.9 0.1 reduce_sum.36
  248.0 8.0 %all_to_all.16 = f32[4,1,256]{2,1,0:T(1,128)S(1)} all-to-all(f32[4,1,256]{2,1,0:T(1,128)S(1)} %broadcast_in_dim.55), channel_id=1, replica_groups=mesh['kv'=4,'seq'=64] {'kv'}, dimensions={0} | all-to-all | bytes 8192 | tf_op jit(solution)/shard_map/all_to_all | solution.py:27
  256.0 0.6 broadcast_multiply_fusion
  (34 shorter events, 0.4 us)
Async XLA Ops:
  6.5 90.8 %all-gather.2.cloned.1.call-start = ((), (), s32[]{:S(2)}) async-start(), calls=%async_computation.2 | async-start | bytes 8519680 | tf_op jit(solution)/shard_map/all_gather | solution.py:73
Sparse Core Ops, SparseCore 0:
  10.2 87.1 all-gather.1
where the time goes:
time: 265 us; the launch traced here: 263 us
  blocking collectives  113 us (43%)
  waiting for transfers between devices  86.6 us (33%)
  loops' own time  21.6 us (8%)
  local copies, waits for them, and re-layouts  14 us (5%)
  between operations  13.5 us (5%)
  matrix products  8.79 us (3%)
  other arithmetic  6.1 us (2%)
    all_to_all x1, blocking collectives, sum_at_owner(): lax.all_to_all(split_up(array, dim, devices), axis, 0, 0, tiled=True)  105 us
    all_gather x1, waiting for transfers between devices, on_device(): gathered = lax.all_gather(key_vectors, 'seq', axis=0, tiled=True)  86.6 us
    another operation x1, loops' own time, terms(): lax.map(portion, jnp.arange(amount // stride, dtype=jnp.int32))  10.7 us
    another operation x1, loops' own time, on_device(): lax.scan(sweep, initial, jnp.arange(total_keys // key_stride, dtype=jnp.i...  10.6 us
    dynamic_slice x16, local copies, waits for them, and re-layouts, on_device(): lax.scan(sweep, initial, jnp.arange(total_keys // key_stride, dtype=jnp.i...  9.59 us
    dot_general x2, matrix products, block_scores(): jnp.einsum('rgid,kgd->rgik', query_block, key_block, preferred_element_ty...  8.79 us
    all_to_all x1, blocking collectives, copy_for_each(): return lax.all_to_all(copies, axis, split_axis=0, concat_axis=0, tiled=True)  7.96 us
  transfers between devices with their start and end apart: 1, of which 1 were waited for; matrix products, arithmetic and copies ran while one was open for 1% of the time, Pallas kernels for 0%

commit v1 on v0

v1 whole, which is shorter than its diff:
```python
import functools
import math

import jax
import jax.numpy as jnp
from jax import lax
from jax.experimental import pallas as pl
from jax.experimental.pallas import tpu as pltpu
from jax.sharding import PartitionSpec as P

HD = 128
SCALE2 = math.log2(math.e) / math.sqrt(HD)
NEG = -1e30
BIG = 2.0**100
NZ, NX = 8, 4
MESH = pl.DeviceIdType.MESH
QB = 256
KC = 2048
KD = 1024
GIVEN = (1, 2, 2, 3)


def place():
    seq = lax.axis_index("seq")
    return lax.axis_index("kv"), seq // 8, lax.rem(seq // 2, 4), lax.rem(seq, 2)


def gather_kernel(q_ref, k_ref, qo_ref, ko_ref, lsem, ssem, rsem):
    y, z, x, c = place()
    width = k_ref.shape[1]
    nq = q_ref.shape[1]

    def dev(zz, xx, cc):
        return (y, (zz * NX + xx) * 2 + cc)

    def zn(d):
        return lax.rem(z + d + NZ, NZ)

    def xn(d):
        return lax.rem(x + d + NX, NX)

    barrier = pltpu.get_barrier_semaphore()
    mirror = NZ - 1 - z
    peers = [dev(z, x, 1 - c)] + [dev(zn(d), x, c) for d in (1, -1)] + [dev(z, xn(d), c) for d in (1, -1)]
    for p in peers:
        pl.semaphore_signal(barrier, inc=1, device_id=p, device_id_type=MESH)
    for cc in (0, 1):
        pl.semaphore_signal(barrier, inc=1, device_id=dev(mirror, x, cc), device_id_type=MESH)
    pl.semaphore_wait(barrier, len(peers) + 2)

    count = [0]
    sends = []

    def send(src, dst, to):
        i = count[0]
        count[0] += 1
        cp = pltpu.make_async_remote_copy(
            src_ref=src, dst_ref=dst, send_sem=ssem.at[i], recv_sem=rsem.at[i], device_id=to, device_id_type=MESH
        )
        cp.start()
        sends.append(cp)
        return cp

    def part(zz, xx, half, piece=None):
        if piece is None:
            return ko_ref.at[zz, xx, half]
        w = width // 2
        return ko_ref.at[zz, xx, half, pl.ds(piece * w, w)]

    pk = send(k_ref.at[1 - c], ko_ref.at[z, x, c], dev(z, x, 1 - c))
    local_k = pltpu.make_async_copy(k_ref.at[c], ko_ref.at[z, x, c], lsem.at[0])
    local_k.start()
    pq = send(q_ref.at[1 - c], qo_ref.at[c], dev(z, x, 1 - c))
    local_q = pltpu.make_async_copy(q_ref.at[c], qo_ref.at[c], lsem.at[1])
    local_q.start()
    local_k.wait()
    pk.wait_recv()

    DIRS = (1, -1)

    def move(zz, xx, half, to, piece=None):
        r = part(zz, xx, half, piece)
        return send(r, r, to)

    ax1 = {d: move(z, x, 0, dev(z, xn(d), c)) for d in DIRS}
    bz = {(1, d): move(z, x, 1, dev(zn(d), x, c)) for d in DIRS}
    az = {}
    bx = {}
    bx2 = {}

    def az_start(step, xd, d):
        zz = zn(-d * (step - 1))
        xx = xn(xd)
        piece = None if step < 4 else (0 if d == 1 else 1)
        az[(step, xd, d)] = move(zz, xx, 0, dev(zn(d), x, c), piece)

    def bz_start(step, d):
        piece = None if step < 4 else (0 if d == 1 else 1)
        bz[(step, d)] = move(zn(-d * (step - 1)), x, 1, dev(zn(d), x, c), piece)

    def bx_start(zd):
        for d in DIRS:
            bx[(zd, d)] = move(zn(zd), x, 1, dev(z, xn(d), c))

    def bx_forward(zd):
        for d in DIRS:
            bx[(zd, d)].wait_recv()
        for d in DIRS:
            bx2[(zd, d)] = move(zn(zd), xn(-d), 1, dev(z, xn(d), c), 0 if d == 1 else 1)

    for d in DIRS:
        az_start(1, 0, d)
    bx_start(0)
    for d in DIRS:
        bz[(1, d)].wait_recv()
        bz_start(2, d)
    bx_start(1)
    bx_start(-1)
    ax2 = {}
    for d in DIRS:
        ax1[d].wait_recv()
    for d in DIRS:
        ax2[d] = move(z, xn(-d), 0, dev(z, xn(d), c), 0 if d == 1 else 1)
    for d in DIRS:
        az_start(1, -1, d)
        az_start(1, 1, d)

    @pl.when((z >= 4) & (c == 1))
    def _():
        for cc in (0, 1):
            pltpu.make_async_remote_copy(
                src_ref=q_ref.at[cc], dst_ref=qo_ref.at[2], send_sem=ssem.at[ssem.shape[0] - 1 - cc],
                recv_sem=rsem.at[rsem.shape[0] - 1], device_id=dev(mirror, x, cc), device_id_type=MESH,
            ).start()

    for d in DIRS:
        bz[(2, d)].wait_recv()
        bz_start(3, d)
    bx_start(2)
    bx_start(-2)
    for d in DIRS:
        ax2[d].wait_recv()
    for d in DIRS:
        az_start(1, 2, d)
    for d in DIRS:
        az[(1, 0, d)].wait_recv()
        az_start(2, 0, d)
    bx_forward(0)
    for d in DIRS:
        bz[(3, d)].wait_recv()
    for d in DIRS:
        bz_start(4, d)
    bx_start(3)
    bx_start(-3)
    for xd in (-1, 1):
        for d in DIRS:
            az[(1, xd, d)].wait_recv()
            az_start(2, xd, d)
    bx_forward(1)
    bx_forward(-1)
    for d in DIRS:
        bz[(4, d)].wait_recv()
    bx_start(4)
    for d in DIRS:
        az[(1, 2, d)].wait_recv()
        az_start(2, 2, d)
    for step, zd in ((2, (2, -2)), (3, (3, -3))):
        for xd in (0, -1):
            for d in DIRS:
                az[(step, xd, d)].wait_recv()
            for d in DIRS:
                az_start(step + 1, xd, d)
        bx_forward(zd[0])
        bx_forward(zd[1])
        for xd in (1, 2):
            for d in DIRS:
                az[(step, xd, d)].wait_recv()
            for d in DIRS:
                az_start(step + 1, xd, d)
    bx_forward(4)
    for xd in (0, -1, 1, 2):
        for d in DIRS:
            az[(4, xd, d)].wait_recv()
    for cp in bx2.values():
        cp.wait_recv()
    pq.wait_recv()
    local_q.wait()
    for cp in sends:
        cp.wait_send()

    @pl.when((z >= 4) & (c == 1))
    def _():
        for cc in (0, 1):
            pltpu.make_async_remote_copy(
                src_ref=q_ref.at[cc], dst_ref=qo_ref.at[2], send_sem=ssem.at[ssem.shape[0] - 1 - cc],
                recv_sem=rsem.at[rsem.shape[0] - 1], device_id=dev(mirror, x, cc), device_id_type=MESH,
            ).wait_send()

    @pl.when(z < 4)
    def _():
        pltpu.make_async_remote_copy(
            src_ref=q_ref.at[0], dst_ref=qo_ref.at[2], send_sem=ssem.at[ssem.shape[0] - 1],
            recv_sem=rsem.at[rsem.shape[0] - 1], device_id=dev(mirror, x, 1), device_id_type=MESH,
        ).wait_recv()


NCOPY = 2 + 4 + 2 + 16 * 2 + 6 + 32


def gather(qh, kh):
    return pl.pallas_call(
        gather_kernel,
        out_shape=(
            jax.ShapeDtypeStruct((3, *qh.shape[1:]), qh.dtype),
            jax.ShapeDtypeStruct((NZ, NX, 2, *kh.shape[1:]), kh.dtype),
        ),
        in_specs=[pl.BlockSpec(memory_space=pl.ANY)] * 2,
        out_specs=(pl.BlockSpec(memory_space=pl.ANY),) * 2,
        scratch_shapes=[
            pltpu.SemaphoreType.DMA((2,)),
            pltpu.SemaphoreType.DMA((NCOPY + 4,)),
            pltpu.SemaphoreType.DMA((NCOPY + 4,)),
        ],
        compiler_params=pltpu.CompilerParams(collective_id=0, has_side_effects=True),
        name="gather_keys",
    )(qh, kh)


def compute_kernel(pos_ref, q_ref, k_ref, out_ref, e_ref, acc_ref, m_ref, z_ref, flag_ref, *, heads):
    _, z, _, _ = place()
    rows = QB // heads
    lower = z < 4
    level = jnp.where(lower, 3 - z, z - 4)
    given = jnp.int32(0)
    for i, g in enumerate(GIVEN):
        given = jnp.where(level == i, g, given)
    blocks = jnp.where(lower, 6 + given, 6 - given)
    acc_ref[...] = jnp.zeros_like(acc_ref)

    def lanes(start, l):
        return pl.ds(pl.multiple_of(start + l * 128, 128), 128)

    def block(i, carry):
        b = jnp.where(i < 6, i, i + 3 - given)
        r0 = b * rows
        lo, hi = pos_ref[r0], pos_ref[r0 + rows - 1]
        wide = (lo + 1) // KC
        narrow = (hi + KD) // KD
        qb = q_ref[pl.ds(pl.multiple_of(b * QB, QB), QB), :]

        def places():
            return jnp.concatenate(
                [jnp.full((heads, 128), pos_ref[r0 + t], jnp.int32) for t in range(rows)], 0
            )

        def scores(start, width):
            keys = k_ref[pl.ds(pl.multiple_of(start, 128), width), :]
            return lax.dot_general(qb, keys, (((1,), (1,)), ((), ())), preferred_element_type=jnp.float32)

        iota = lax.broadcasted_iota(jnp.int32, (QB, 128), 1)
        first = jnp.max(jnp.where(iota <= places(), scores(0, 128), NEG), axis=1, keepdims=True)
        m_ref[...] = jnp.broadcast_to(first * SCALE2, (QB, 128))

        def attempt(a, carry):
            @pl.when((a == 0) | (flag_ref[0] == 1))
            def _():
                def sweep(width, masked):
                    def body(c, total):
                        start = pl.multiple_of(c * width, width)
                        s = scores(start, width)
                        shift = m_ref[...]
                        if masked:
                            seen = places()
                        for l in range(width // 128):
                            e = jnp.exp2(s[:, l * 128 : (l + 1) * 128] * SCALE2 - shift)
                            if masked:
                                e = jnp.where(iota + (start + l * 128) <= seen, e, 0.0)
                            e_ref[:, lanes(start, l)] = e
                            total = total + e
                        return total

                    return body

                total = jnp.zeros((QB, 128), jnp.float32)
                total = lax.fori_loop(0, wide, sweep(KC, False), total)
                total = lax.fori_loop(wide * (KC // KD), narrow, sweep(KD, True), total)
                total = jnp.sum(total, axis=1, keepdims=True)
                z_ref[...] = jnp.broadcast_to(1.0 / total, (QB, 128))
                over = jnp.logical_not(jnp.max(total) <= BIG)
                flag_ref[0] = over.astype(jnp.int32)

                @pl.when(over & (a == 0))
                def _():
                    def largest(c, best):
                        start = pl.multiple_of(c * KD, KD)
                        s = scores(start, KD)
                        seen = places()
                        for l in range(KD // 128):
                            part = s[:, l * 128 : (l + 1) * 128]
                            best = jnp.maximum(best, jnp.where(iota + (start + l * 128) <= seen, part, NEG))
                        return best

                    best = lax.fori_loop(0, narrow, largest, jnp.full((QB, 128), NEG, jnp.float32))
                    m_ref[...] = jnp.broadcast_to(jnp.max(best, axis=1, keepdims=True) * SCALE2, (QB, 128))

            return carry

        lax.fori_loop(0, 2, attempt, 0)

        def columns(c, carry):
            start = pl.multiple_of(c * KD, KD)
            sums = [acc_ref[:, lanes(start, l)] for l in range(KD // 128)]
            for t in range(QB // 8):
                weight = z_ref[8 * t : 8 * t + 8]
                for l in range(KD // 128):
                    sums[l] = sums[l] + e_ref[8 * t : 8 * t + 8, lanes(start, l)] * weight
            for l in range(KD // 128):
                acc_ref[:, lanes(start, l)] = sums[l]
            return carry

        lax.fori_loop(0, narrow, columns, 0)
        return carry

    lax.fori_loop(0, blocks, block, 0)
    for zz in range(8):
        out_ref[zz] = jnp.concatenate(
            [jnp.sum(acc_ref[:, pl.ds(zz * 2048 + r * 256, 256)], axis=0, keepdims=True) for r in range(8)], 0
        )


def compute(places, q, k, heads):
    keys = k.shape[0]
    return pl.pallas_call(
        functools.partial(compute_kernel, heads=heads),
        out_shape=jax.ShapeDtypeStruct((8, 8, keys // 64), jnp.float32),
        in_specs=[pl.BlockSpec(memory_space=pltpu.SMEM)] + [pl.BlockSpec(memory_space=pltpu.VMEM)] * 2,
        out_specs=pl.BlockSpec(memory_space=pltpu.VMEM),
        scratch_shapes=[
            pltpu.VMEM((QB, keys), jnp.float32),
            pltpu.VMEM((8, keys), jnp.float32),
            pltpu.VMEM((QB, 128), jnp.float32),
            pltpu.VMEM((QB, 128), jnp.float32),
            pltpu.SMEM((1,), jnp.int32),
        ],
        compiler_params=pltpu.CompilerParams(vmem_limit_bytes=48 << 20),
        name="key_scores",
    )(places, q, k)


def reduce_kernel(p_ref, out_ref, bz, bx, by, mine, mine2, ssem, rsem, *, factor):
    y, z, x, c = place()
    xc = x * 2 + c

    def dev(yy, zz, w):
        return (yy, zz * 8 + w)

    def others(i, n, d):
        return lax.rem(i + d, n)

    zs = [dev(y, others(z, 8, d), xc) for d in range(1, 8)]
    xs = [dev(y, z, others(xc, 8, d)) for d in range(1, 8)]
    ys = [dev(others(y, 4, d), z, xc) for d in range(1, 4)]
    barrier = pltpu.get_barrier_semaphore()
    for p in zs + xs + ys:
        pl.semaphore_signal(barrier, inc=1, device_id=p, device_id_type=MESH)
    pl.semaphore_wait(barrier, len(zs + xs + ys))

    def exchange(srcs, dst, peers, base):
        cps = []
        for i, (s, p) in enumerate(zip(srcs, peers)):
            cp = pltpu.make_async_remote_copy(
                src_ref=s, dst_ref=dst.at[i], send_sem=ssem.at[base + i], recv_sem=rsem.at[base + i],
                device_id=p, device_id_type=MESH,
            )
            cp.start()
            cps.append(cp)
        for cp in cps:
            cp.wait_recv()
        return cps

    cps = exchange([p_ref.at[others(z, 8, d)] for d in range(1, 8)], bz, zs, 0)
    total = p_ref[z]
    for i in range(7):
        total = total + bz[i]
    mine[...] = total
    cps += exchange([mine] * 7, bx, xs, 7)
    for i in range(7):
        total = total + bx[i]
    mine2[...] = total
    cps += exchange([mine2] * 3, by, ys, 14)
    for i in range(3):
        total = total + by[i]
    rows = lax.broadcasted_iota(jnp.int32, total.shape, 0)
    out_ref[...] = jnp.sum(jnp.where(rows == xc, total, 0.0), axis=0, keepdims=True) * factor
    for cp in cps:
        cp.wait_send()


def reduce(partial, factor):
    tile = partial.shape[1:]
    return pl.pallas_call(
        functools.partial(reduce_kernel, factor=factor),
        out_shape=jax.ShapeDtypeStruct((1, tile[1]), jnp.float32),
        in_specs=[pl.BlockSpec(memory_space=pltpu.VMEM)],
        out_specs=pl.BlockSpec(memory_space=pltpu.VMEM),
        scratch_shapes=[
            pltpu.VMEM((7, *tile), jnp.float32),
            pltpu.VMEM((7, *tile), jnp.float32),
            pltpu.VMEM((3, *tile), jnp.float32),
            pltpu.VMEM(tile, jnp.float32),
            pltpu.VMEM(tile, jnp.float32),
            pltpu.SemaphoreType.DMA((17,)),
            pltpu.SemaphoreType.DMA((17,)),
        ],
        compiler_params=pltpu.CompilerParams(collective_id=1, has_side_effects=True),
        name="sum_scores",
    )(partial)


def on_device(sampled_rows, query_vectors, key_vectors):
    rows, all_heads, _ = query_vectors.shape
    groups = key_vectors.shape[1]
    heads = all_heads // groups
    _, z, x, _ = place()
    qh = query_vectors.reshape(rows, groups, heads * HD).transpose(1, 0, 2).reshape(groups, rows * heads, HD)
    kh = key_vectors.transpose(1, 0, 2)
    own = lax.dynamic_slice_in_dim(sampled_rows, (z * NX + x) * 2 * rows, 2 * rows, 0)
    lent = lax.dynamic_slice_in_dim(sampled_rows, ((7 - z) * NX + x) * 2 * rows + rows, rows, 0)
    places = jnp.concatenate([own, lent])
    q, k = gather(qh, kh)
    partial = compute(places, q.reshape(-1, HD), k.reshape(-1, HD), heads)
    return reduce(partial, 1.0 / heads).reshape(-1)


def solution(mesh):
    placed = (P(), P("seq", "kv", None), P("seq", "kv", None))
    return jax.shard_map(on_device, mesh=mesh, in_specs=placed, out_specs=P("seq"), check_vma=False)
```

time: 265 us -> 155 us (0.58)
  Pallas kernels: 0 us -> 144 us
  blocking collectives: 113 us -> 0 us
  waiting for transfers between devices: 86.6 us -> 0 us
  loops' own time: 21.6 us -> 0 us
  between operations: 13.5 us -> 0.06 us
  matrix products: 8.79 us -> 0 us
  other arithmetic: 6.1 us -> 0.08 us
  local copies, waits for them, and re-layouts: 14 us -> 10.3 us
    pallas_call x0 -> x3, Pallas kernels: none -> 144 us  [the longest x1 50.6 us: reduce(): pl.pallas_call(functools.partial(reduce_kernel, factor=factor), out_shape...]
    all_to_all x2 -> x0, blocking collectives: 113 us -> none  [the longest x1 105 us: sum_at_owner(): lax.all_to_all(split_up(array, dim, devices), axis, 0, 0, tiled=True)]
    all_gather x1 -> x0, waiting for transfers between devices: 86.6 us -> none  [on_device(): gathered = lax.all_gather(key_vectors, 'seq', axis=0, tiled=True)]
    another operation x18 -> x0, loops' own time: 21.6 us -> none  [the longest x1 10.7 us: terms(): lax.map(portion, jnp.arange(amount // stride, dtype=jnp.int32))]
    dot_general x2 -> x0, matrix products: 8.79 us -> none  [block_scores(): jnp.einsum('rgid,kgd->rgik', query_block, key_block, preferred_element_ty...]
    dynamic_slice x16 -> x2, local copies, waits for them, and re-layouts: 9.59 us -> 1.53 us  [the longest x1 0.77 us: on_device(): lax.dynamic_slice_in_dim(sampled_rows, (z * NX + x) * 2 * rows, 2 * rows, 0)]
    unnamed x2 -> x8, local copies, waits for them, and re-layouts: 2.67 us -> 6.64 us
    reduce_sum x3 -> x0, other arithmetic: 3.66 us -> none  [the longest x1 3.55 us: stats_block(): jnp.sum(terms, axis=-1)]
  transfers between devices with their start and end apart: 1 -> 0, of which waited for: 1 -> 0; matrix products, arithmetic and copies ran while one was open for 1% -> 0% of each run, Pallas kernels for 0% -> 0%
where the time goes in v1:
time: 155 us; the launch traced here: 154 us
  Pallas kernels  144 us (93%)
  local copies, waits for them, and re-layouts  10.3 us (7%)
    pallas_call x1, Pallas kernels, reduce(): pl.pallas_call(functools.partial(reduce_kernel, factor=factor), out_shape...  50.6 us
    pallas_call x1, Pallas kernels, gather(): pl.pallas_call(gather_kernel, out_shape=(jax.ShapeDtypeStruct((3, *qh.sha...  50.3 us
    pallas_call x1, Pallas kernels, compute(): pl.pallas_call(functools.partial(compute_kernel, heads=heads), out_shape=...  43.1 us
    unnamed x8, local copies, waits for them, and re-layouts  6.64 us

profile of v1, /device:TPU:1, one launch (start us, length us, event | category | flops | bytes accessed | tf_op | source)
XLA Modules:
  0.0 154.4 jit_solution(4198967558565229243)
XLA Ops:
  0.0 0.8 dynamic_slice.7
  0.8 0.8 dynamic_slice.6
  1.5 0.1 pad_add_fusion.pos_ref
  1.6 1.6 %copy.9 = bf16[256,2,128]{2,0,1:T(8,128)(2,1)} copy(bf16[256,2,128]{2,1,0:T(2,128)(2,1)} %param.5) | data formatting | bytes 262144 | tf_op args[2]
  3.2 1.1 reshape.15
  4.3 0.1 copy.8
  4.3 0.9 reshape.16.q_ref
  5.3 50.3 %gather_keys.1 = (bf16[3,768,128]{2,1,0:T(8,128)(2,1)}, bf16[8,4,2,256,128]{4,3,2,1,0:T(8,128)(2,1)}) custom-call(bf16[2,768,128]{2,1,0:T(8,128)(2,1)} %reshape.16.q_ref, bf16[2,256,128]{2,1,0:T(8,128)(2,1)} %bitcast.12), custom_call_target="tpu_custom_call" | custom-call | tf_op jit(solution)/shard_map/gather_keys/pallas_call | solution.py:211
  55.6 0.0 copy-start
  55.6 2.2 %copy-done = bf16[8,4,2,256,128]{4,3,2,1,0:T(8,128)(2,1)S(1)} copy-done((bf16[8,4,2,256,128]{4,3,2,1,0:T(8,128)(2,1)S(1)}, bf16[8,4,2,256,128]{4,3,2,1,0:T(8,128)(2,1)}, u32[]{:S(2)}) %copy-start) | copy-done | bytes 4194328
  57.8 0.0 copy-start.1
  57.8 1.1 copy-done.1
  58.9 43.1 %key_scores.1.p_ref = f32[8,8,256]{2,1,0:T(8,128)S(1)} custom-call(s32[288]{0:T(512)S(1)} %pad_add_fusion.pos_ref, bf16[2304,128]{1,0:T(8,128)(2,1)S(1)} %bitcast.10, bf16[16384,128]{1,0:T(8,128)(2,1)S(1)} %bitcast.9), custom_call_target="tpu_custom_call" | custom-call | tf_op jit(solution)/shard_map/key_scores/pallas_call | solution.py:333
  101.9 0.0 copy-start.2
  102.0 0.6 copy-done.2
  102.6 50.6 %sum_scores.1 = f32[1,256]{1,0:T(1,128)} custom-call(f32[8,8,256]{2,1,0:T(8,128)} %copy-done.2), custom_call_target="tpu_custom_call" | custom-call | tf_op jit(solution)/shard_map/sum_scores/pallas_call | solution.py:401
  153.2 1.2 copy.11
Async XLA Ops:
  55.6 2.2 %copy-start = (bf16[8,4,2,256,128]{4,3,2,1,0:T(8,128)(2,1)S(1)}, bf16[8,4,2,256,128]{4,3,2,1,0:T(8,128)(2,1)}, u32[]{:S(2)}) copy-start(bf16[8,4,2,256,128]{4,3,2,1,0:T(8,128)(2,1)} %get-tuple-element.8) | copy-start | bytes 12582916
  57.8 1.1 copy-start.1
  101.9 0.6 copy-start.2

commit v2 on v1

v2 whole, which is shorter than its diff:
```python
import functools
import math

import jax
import jax.numpy as jnp
from jax import lax
from jax.experimental import pallas as pl
from jax.experimental.pallas import tpu as pltpu
from jax.sharding import PartitionSpec as P

HD = 128
SCALE2 = math.log2(math.e) / math.sqrt(HD)
NEG = -1e30
BIG = 2.0**100
NZ, NX = 8, 4
MESH = pl.DeviceIdType.MESH
QB = 256
WIDE = 16
NARROW = 4
DIRS = (1, -1)


def place():
    seq = lax.axis_index("seq")
    return lax.axis_index("kv"), seq // 8, lax.rem(seq // 2, 4), lax.rem(seq, 2)


def gather_kernel(q_ref, k_ref, qo_ref, ko_ref, lsem, ssem, rsem):
    y, z, x, c = place()
    head = lax.rem(z, 2)
    half = k_ref.shape[1] // 2

    def dev(zz, xx, cc):
        return (y, (zz * NX + xx) * 2 + cc)

    def zn(d):
        return lax.rem(z + d + NZ, NZ)

    def xn(d):
        return lax.rem(x + d + NX, NX)

    partner = dev(z, x, 1 - c)
    mirror = dev(NZ - 1 - z, x, c)
    barrier = pltpu.get_barrier_semaphore()
    peers = [partner, mirror]
    peers += [dev(zn(d), x, c) for d in (1, -1, 2, -2, 3, -3)]
    peers += [dev(z, xn(d), c) for d in DIRS]
    for p in peers:
        pl.semaphore_signal(barrier, inc=1, device_id=p, device_id_type=MESH)
    local_k = pltpu.make_async_copy(k_ref.at[head], ko_ref.at[z, x, c], lsem.at[0])
    local_k.start()
    local_q = pltpu.make_async_copy(q_ref.at[:, head], qo_ref.at[0], lsem.at[1])
    local_q.start()
    pl.semaphore_wait(barrier, len(peers))

    sends = []

    def send(src, dst, to):
        i = len(sends)
        cp = pltpu.make_async_remote_copy(
            src_ref=src, dst_ref=dst, send_sem=ssem.at[i], recv_sem=rsem.at[i], device_id=to, device_id_type=MESH
        )
        cp.start()
        sends.append(cp)
        return cp

    def block(zz, xx, piece=None):
        ref = ko_ref.at[zz, xx, c]
        return ref if piece is None else ref.at[pl.ds(piece * half, half)]

    def move(zz, xx, to, piece=None):
        r = block(zz, xx, piece)
        return send(r, r, to)

    mine = block(z, x)
    ax = {}
    az = {}
    for d in DIRS:
        az[d] = send(k_ref.at[1 - head], mine, dev(zn(d), x, c))
        ax[(0, d)] = send(k_ref.at[head], mine, dev(z, xn(d), c))
    for d in DIRS:
        az[2 * d] = send(k_ref.at[head], mine, dev(zn(2 * d), x, c))
    for d in DIRS:
        az[3 * d] = send(k_ref.at[1 - head], mine, dev(zn(3 * d), x, c))
    twin = [send(k_ref.at[head], mine, partner)]
    fx = {}

    def spread(zd):
        zz = zn(zd)
        for d in DIRS:
            ax[(zd, d)] = move(zz, x, dev(z, xn(d), c))
        twin.append(move(zz, x, partner))

    def forward(zd):
        zz = zn(zd)
        for d in DIRS:
            ax[(zd, d)].wait_recv()
        for d in DIRS:
            fx[(zd, d)] = move(zz, xn(-d), dev(z, xn(d), c), 0 if d == 1 else 1)
        for d in DIRS:
            twin.append(move(zz, xn(-d), partner))

    def finish(zd):
        for d in DIRS:
            fx[(zd, d)].wait_recv()
        twin.append(move(zn(zd), xn(2), partner))

    for d in DIRS:
        az[-d].wait_recv()
        spread(d)
    forward(0)
    for d in DIRS:
        az[-2 * d].wait_recv()
    far = {d: move(zn(2 * d), x, dev(zn(-2 * d), x, c), 0 if d == 1 else 1) for d in DIRS}
    for d in DIRS:
        spread(2 * d)
    swap = send(q_ref.at[:, 1 - head], qo_ref.at[1], mirror)
    for d in DIRS:
        forward(d)
    for d in DIRS:
        az[-3 * d].wait_recv()
        spread(3 * d)
    finish(0)
    for d in DIRS:
        forward(2 * d)
    for d in DIRS:
        far[d].wait_recv()
    spread(4)
    for d in DIRS:
        finish(d)
    for d in DIRS:
        forward(3 * d)
    for d in DIRS:
        finish(2 * d)
    forward(4)
    for d in DIRS:
        finish(3 * d)
    finish(4)
    local_k.wait()
    local_q.wait()
    swap.wait_recv()
    for cp in twin:
        cp.wait_recv()
    for cp in sends:
        cp.wait_send()


COPIES = 73


def gather(q, k):
    rows, _, heads, hd = q.shape
    return pl.pallas_call(
        gather_kernel,
        out_shape=(
            jax.ShapeDtypeStruct((2, rows, heads, hd), q.dtype),
            jax.ShapeDtypeStruct((NZ, NX, 2, *k.shape[1:]), k.dtype),
        ),
        in_specs=[pl.BlockSpec(memory_space=pl.ANY)] * 2,
        out_specs=(pl.BlockSpec(memory_space=pltpu.VMEM),) * 2,
        scratch_shapes=[
            pltpu.SemaphoreType.DMA((2,)),
            pltpu.SemaphoreType.DMA((COPIES,)),
            pltpu.SemaphoreType.DMA((COPIES,)),
        ],
        compiler_params=pltpu.CompilerParams(collective_id=0, has_side_effects=True, vmem_limit_bytes=16 << 20),
        name="gather_keys",
    )(q, k)


def compute_kernel(pos_ref, q_ref, k_ref, out_ref, e_ref, acc_ref, m_ref, w_ref, z_ref, flag_ref, *, heads):
    _, z, x, c = place()
    rows = QB // heads
    per = pos_ref.shape[0] // (NZ * NX * 2)
    each = per // rows
    width = k_ref.shape[2]
    tiles = width // 128
    acc_ref[...] = jnp.zeros_like(acc_ref)

    def block(i, carry):
        plane = jnp.where(i < each, z, NZ - 1 - z)
        r0 = ((plane * NX + x) * 2 + c) * per + lax.rem(i, each) * rows
        lo, hi = pos_ref[r0], pos_ref[r0 + rows - 1]
        wide = (lo + 1) // (WIDE * width)
        open_end = (lo + 1) // (NARROW * width)
        end = hi // (NARROW * width) + 1
        qb = q_ref[pl.ds(pl.multiple_of(i * QB, QB), QB), :]

        def places():
            return jnp.concatenate(
                [jnp.full((heads, 128), pos_ref[r0 + t], jnp.int32) for t in range(rows)], 0
            )

        iota = lax.broadcasted_iota(jnp.int32, (QB, 128), 1)
        first = jnp.dot(qb, k_ref[0, :, 0:128], preferred_element_type=jnp.float32)
        first = jnp.max(jnp.where(iota <= places(), first, NEG), axis=1, keepdims=True)
        m_ref[...] = jnp.broadcast_to(first * SCALE2, (QB, 128))

        def attempt(a, carry):
            @pl.when((a == 0) | (flag_ref[0] == 1))
            def _():
                z_ref[...] = jnp.zeros_like(z_ref)

                def sweep(count, masked):
                    def body(step, carry):
                        total = None
                        for g in range(count):
                            b = step * count + g
                            s = jnp.dot(qb, k_ref[b], preferred_element_type=jnp.float32)
                            for l in range(tiles):
                                e = jnp.exp2(s[:, l * 128 : (l + 1) * 128] * SCALE2 - m_ref[...])
                                if masked:
                                    e = jnp.where(iota + (b * width + l * 128) <= places(), e, 0.0)
                                e_ref[b * tiles + l] = e
                                total = e if total is None else total + e
                        z_ref[...] += total
                        return carry

                    return body

                lax.fori_loop(0, wide, sweep(WIDE, False), 0)
                lax.fori_loop(wide * (WIDE // NARROW), open_end, sweep(NARROW, False), 0)
                lax.fori_loop(open_end, end, sweep(NARROW, True), 0)
                total = jnp.sum(z_ref[...], axis=1, keepdims=True)
                w_ref[...] = jnp.broadcast_to(1.0 / total, (QB, 128))
                over = jnp.logical_not(jnp.max(total) <= BIG)
                flag_ref[0] = over.astype(jnp.int32)

                @pl.when(over & (a == 0))
                def _():
                    def largest(b, best):
                        s = jnp.dot(qb, k_ref[b], preferred_element_type=jnp.float32)
                        for l in range(tiles):
                            seen = iota + (b * width + l * 128) <= places()
                            best = jnp.maximum(best, jnp.where(seen, s[:, l * 128 : (l + 1) * 128], NEG))
                        return best

                    best = lax.fori_loop(0, end * NARROW, largest, jnp.full((QB, 128), NEG, jnp.float32))
                    m_ref[...] = jnp.broadcast_to(jnp.max(best, axis=1, keepdims=True) * SCALE2, (QB, 128))

            return carry

        lax.fori_loop(0, 2, attempt, 0)

        def columns(step, carry):
            for g in range(0, NARROW * tiles, 4):
                b = step * (NARROW * tiles) + g
                sums = [acc_ref[b + l] for l in range(4)]
                for t in range(QB // 8):
                    weight = w_ref[8 * t : 8 * t + 8]
                    for l in range(4):
                        sums[l] = sums[l] + e_ref[b + l, 8 * t : 8 * t + 8, :] * weight
                for l in range(4):
                    acc_ref[b + l] = sums[l]
            return carry

        lax.fori_loop(0, end, columns, 0)
        return carry

    lax.fori_loop(0, q_ref.shape[0] // QB, block, 0)
    for zz in range(8):
        for l in range(tiles):
            out_ref[zz, :, l * 128 : (l + 1) * 128] = jnp.concatenate(
                [jnp.sum(acc_ref[(zz * 8 + r) * tiles + l], axis=0, keepdims=True) for r in range(8)], 0
            )


def compute(places, q, k, heads):
    blocks, _, width = k.shape
    return pl.pallas_call(
        functools.partial(compute_kernel, heads=heads),
        out_shape=jax.ShapeDtypeStruct((8, 8, width), jnp.float32),
        in_specs=[pl.BlockSpec(memory_space=pltpu.SMEM)] + [pl.BlockSpec(memory_space=pltpu.VMEM)] * 2,
        out_specs=pl.BlockSpec(memory_space=pltpu.VMEM),
        scratch_shapes=[
            pltpu.VMEM((blocks * width // 128, QB, 128), jnp.float32),
            pltpu.VMEM((blocks * width // 128, 8, 128), jnp.float32),
            pltpu.VMEM((QB, 128), jnp.float32),
            pltpu.VMEM((QB, 128), jnp.float32),
            pltpu.VMEM((QB, 128), jnp.float32),
            pltpu.SMEM((1,), jnp.int32),
        ],
        compiler_params=pltpu.CompilerParams(vmem_limit_bytes=40 << 20),
        name="key_scores",
    )(places, q, k)


def reduce_kernel(p_ref, out_ref, bz, bx, by, mine, mine2, ssem, rsem, *, factor):
    y, z, x, c = place()
    xc = x * 2 + c

    def dev(yy, zz, w):
        return (yy, zz * 8 + w)

    def others(i, n, d):
        return lax.rem(i + d, n)

    zs = [dev(y, others(z, 8, d), xc) for d in range(1, 8)]
    xs = [dev(y, z, others(xc, 8, d)) for d in range(1, 8)]
    ys = [dev(others(y, 4, d), z, xc) for d in range(1, 4)]
    barrier = pltpu.get_barrier_semaphore()
    for p in zs + xs + ys:
        pl.semaphore_signal(barrier, inc=1, device_id=p, device_id_type=MESH)
    pl.semaphore_wait(barrier, len(zs + xs + ys))

    def exchange(srcs, dst, peers, base):
        cps = []
        for i, (s, p) in enumerate(zip(srcs, peers)):
            cp = pltpu.make_async_remote_copy(
                src_ref=s, dst_ref=dst.at[i], send_sem=ssem.at[base + i], recv_sem=rsem.at[base + i],
                device_id=p, device_id_type=MESH,
            )
            cp.start()
            cps.append(cp)
        for cp in cps:
            cp.wait_recv()
        return cps

    cps = exchange([p_ref.at[others(z, 8, d)] for d in range(1, 8)], bz, zs, 0)
    total = p_ref[z]
    for i in range(7):
        total = total + bz[i]
    mine[...] = total
    cps += exchange([mine] * 7, bx, xs, 7)
    for i in range(7):
        total = total + bx[i]
    mine2[...] = total
    cps += exchange([mine2] * 3, by, ys, 14)
    for i in range(3):
        total = total + by[i]
    rows = lax.broadcasted_iota(jnp.int32, total.shape, 0)
    out_ref[...] = jnp.sum(jnp.where(rows == xc, total, 0.0), axis=0, keepdims=True) * factor
    for cp in cps:
        cp.wait_send()


def reduce(partial, factor):
    tile = partial.shape[1:]
    return pl.pallas_call(
        functools.partial(reduce_kernel, factor=factor),
        out_shape=jax.ShapeDtypeStruct((1, tile[1]), jnp.float32),
        in_specs=[pl.BlockSpec(memory_space=pltpu.VMEM)],
        out_specs=pl.BlockSpec(memory_space=pltpu.VMEM),
        scratch_shapes=[
            pltpu.VMEM((7, *tile), jnp.float32),
            pltpu.VMEM((7, *tile), jnp.float32),
            pltpu.VMEM((3, *tile), jnp.float32),
            pltpu.VMEM(tile, jnp.float32),
            pltpu.VMEM(tile, jnp.float32),
            pltpu.SemaphoreType.DMA((17,)),
            pltpu.SemaphoreType.DMA((17,)),
        ],
        compiler_params=pltpu.CompilerParams(collective_id=1, has_side_effects=True),
        name="sum_scores",
    )(partial)


def on_device(sampled_rows, query_vectors, key_vectors):
    rows, all_heads, hd = query_vectors.shape
    groups = key_vectors.shape[1]
    heads = all_heads // groups
    q, k = gather(query_vectors.reshape(rows, groups, heads, hd), key_vectors.transpose(1, 2, 0))
    partial = compute(sampled_rows, q.reshape(-1, hd), k.reshape(-1, *k.shape[3:]), heads)
    return reduce(partial, 1.0 / heads).reshape(-1)


def solution(mesh):
    placed = (P(), P("seq", "kv", None), P("seq", "kv", None))
    return jax.shard_map(on_device, mesh=mesh, in_specs=placed, out_specs=P("seq"), check_vma=False)
```

time: 155 us -> 131 us (0.85)
  Pallas kernels: 144 us -> 126 us
  local copies, waits for them, and re-layouts: 10.3 us -> 4.57 us
    pallas_call x1, Pallas kernels: 50.6 us -> 26.7 us  [reduce(): pl.pallas_call(functools.partial(reduce_kernel, factor=factor), out_shape...]
    pallas_call x1, Pallas kernels: 43.1 us -> 65.3 us  [compute(): pl.pallas_call(functools.partial(compute_kernel, heads=heads), out_shape=...]
    pallas_call x1, Pallas kernels: 50.3 us -> 34.2 us  [gather(): pl.pallas_call(gather_kernel, out_shape=(jax.ShapeDtypeStruct((2, rows, h...]
    reshape x3 -> x0, local copies, waits for them, and re-layouts: 2.11 us -> none  [on_device(): query_vectors.reshape(rows, groups, heads * HD).transpose(1, 0, 2)]
    unnamed x8, local copies, waits for them, and re-layouts: 6.64 us -> 4.57 us
where the time goes in v2:
time: 131 us
  Pallas kernels  126 us (96%)
  local copies, waits for them, and re-layouts  4.57 us (3%)
    pallas_call x1, Pallas kernels, compute(): pl.pallas_call(functools.partial(compute_kernel, heads=heads), out_shape=...  65.3 us
    pallas_call x1, Pallas kernels, gather(): pl.pallas_call(gather_kernel, out_shape=(jax.ShapeDtypeStruct((2, rows, h...  34.2 us
    pallas_call x1, Pallas kernels, reduce(): pl.pallas_call(functools.partial(reduce_kernel, factor=factor), out_shape...  26.7 us
    unnamed x8, local copies, waits for them, and re-layouts  4.57 us

profile of v2, /device:TPU:1, one launch (start us, length us, event | category | flops | bytes accessed | tf_op | source)
XLA Modules:
  0.0 130.8 jit_solution(3772310950921394792)
XLA Ops:
  0.0 1.0 copy.4
  1.0 0.0 copy-start
  1.0 1.0 copy-done
  2.0 34.2 %gather_keys.1 = (bf16[2,96,8,128]{3,2,1,0:T(8,128)(2,1)S(1)}, bf16[8,4,2,128,256]{4,3,2,1,0:T(8,128)(2,1)S(1)}) custom-call(bf16[96,2,8,128]{3,2,1,0:T(8,128)(2,1)S(1)} %bitcast.8, bf16[2,128,256]{2,1,0:T(8,128)(2,1)S(1)} %bitcast.6), custom_call_target="tpu_custom_call" | custom-call | tf_op jit(solution)/shard_map/gather_keys/pallas_call | solution.py:153
  36.2 0.0 copy-start.2
  36.2 0.7 copy-done.2
  37.0 65.3 %key_scores.1.p_ref = f32[8,8,256]{2,1,0:T(8,128)S(1)} custom-call(s32[6144]{0:T(1024)S(1)} %copy-done.2, bf16[1536,128]{1,0:T(8,128)(2,1)S(1)} %bitcast.7, bf16[64,128,256]{2,1,0:T(8,128)(2,1)S(1)} %bitcast.5), custom_call_target="tpu_custom_call" | custom-call | tf_op jit(solution)/shard_map/key_scores/pallas_call | solution.py:270
  102.3 0.0 copy-start.1
  102.3 0.6 copy-done.1
  102.9 26.7 %sum_scores.1 = f32[1,256]{1,0:T(1,128)} custom-call(f32[8,8,256]{2,1,0:T(8,128)} %copy-done.1), custom_call_target="tpu_custom_call" | custom-call | tf_op jit(solution)/shard_map/sum_scores/pallas_call | solution.py:339
  129.6 1.2 copy.6
Async XLA Ops:
  1.0 1.0 copy-start
  36.2 0.7 copy-start.2
  102.3 0.6 copy-start.1

commit v3 on v2

v3 whole, which is shorter than its diff:
```python
import functools
import math

import jax
import jax.numpy as jnp
from jax import lax
from jax.experimental import pallas as pl
from jax.experimental.pallas import tpu as pltpu
from jax.sharding import PartitionSpec as P

HD = 128
SCALE2 = math.log2(math.e) / math.sqrt(HD)
NEG = -1e30
BIG = 2.0**100
NZ, NX = 8, 4
MESH = pl.DeviceIdType.MESH
QB = 256
BLOCKS = 2
STEP = 8
MASKED = 4
DIRS = (1, -1)


def place():
    seq = lax.axis_index("seq")
    return lax.axis_index("kv"), seq // 8, lax.rem(seq // 2, 4), lax.rem(seq, 2)


def gather_kernel(q_ref, k_ref, qo_ref, ko_ref, lsem, ssem, rsem):
    y, z, x, c = place()
    head = lax.rem(z, 2)
    half = k_ref.shape[1] // 2

    def dev(zz, xx, cc):
        return (y, (zz * NX + xx) * 2 + cc)

    def zn(d):
        return lax.rem(z + d + NZ, NZ)

    def xn(d):
        return lax.rem(x + d + NX, NX)

    partner = dev(z, x, 1 - c)
    mirror = dev(NZ - 1 - z, x, c)
    barrier = pltpu.get_barrier_semaphore()
    peers = [partner, mirror]
    peers += [dev(zn(d), x, c) for d in (1, -1, 2, -2, 3, -3)]
    peers += [dev(z, xn(d), c) for d in DIRS]
    for p in peers:
        pl.semaphore_signal(barrier, inc=1, device_id=p, device_id_type=MESH)
    local_k = pltpu.make_async_copy(k_ref.at[head], ko_ref.at[z, x, c], lsem.at[0])
    local_k.start()
    local_q = pltpu.make_async_copy(q_ref.at[:, head], qo_ref.at[0], lsem.at[1])
    local_q.start()
    pl.semaphore_wait(barrier, len(peers))

    sends = []

    def send(src, dst, to):
        i = len(sends)
        cp = pltpu.make_async_remote_copy(
            src_ref=src, dst_ref=dst, send_sem=ssem.at[i], recv_sem=rsem.at[i], device_id=to, device_id_type=MESH
        )
        cp.start()
        sends.append(cp)
        return cp

    def block(zz, xx, piece=None):
        ref = ko_ref.at[zz, xx, c]
        return ref if piece is None else ref.at[pl.ds(piece * half, half)]

    def move(zz, xx, to, piece=None):
        r = block(zz, xx, piece)
        return send(r, r, to)

    mine = block(z, x)
    ax = {}
    az = {}
    for d in DIRS:
        az[d] = send(k_ref.at[1 - head], mine, dev(zn(d), x, c))
        ax[(0, d)] = send(k_ref.at[head], mine, dev(z, xn(d), c))
    for d in DIRS:
        az[2 * d] = send(k_ref.at[head], mine, dev(zn(2 * d), x, c))
    for d in DIRS:
        az[3 * d] = send(k_ref.at[1 - head], mine, dev(zn(3 * d), x, c))
    twin = [send(k_ref.at[head], mine, partner)]
    fx = {}

    def spread(zd):
        zz = zn(zd)
        for d in DIRS:
            ax[(zd, d)] = move(zz, x, dev(z, xn(d), c))
        twin.append(move(zz, x, partner))

    def forward(zd):
        zz = zn(zd)
        for d in DIRS:
            ax[(zd, d)].wait_recv()
        for d in DIRS:
            fx[(zd, d)] = move(zz, xn(-d), dev(z, xn(d), c), 0 if d == 1 else 1)
        for d in DIRS:
            twin.append(move(zz, xn(-d), partner))

    def finish(zd):
        for d in DIRS:
            fx[(zd, d)].wait_recv()
        twin.append(move(zn(zd), xn(2), partner))

    for d in DIRS:
        az[-d].wait_recv()
        spread(d)
    forward(0)
    for d in DIRS:
        az[-2 * d].wait_recv()
    far = {d: move(zn(2 * d), x, dev(zn(-2 * d), x, c), 0 if d == 1 else 1) for d in DIRS}
    for d in DIRS:
        spread(2 * d)
    swap = send(q_ref.at[:, 1 - head], qo_ref.at[1], mirror)
    for d in DIRS:
        forward(d)
    for d in DIRS:
        az[-3 * d].wait_recv()
        spread(3 * d)
    finish(0)
    for d in DIRS:
        forward(2 * d)
    for d in DIRS:
        far[d].wait_recv()
    spread(4)
    for d in DIRS:
        finish(d)
    for d in DIRS:
        forward(3 * d)
    for d in DIRS:
        finish(2 * d)
    forward(4)
    for d in DIRS:
        finish(3 * d)
    finish(4)
    local_k.wait()
    local_q.wait()
    swap.wait_recv()
    for cp in twin:
        cp.wait_recv()
    for cp in sends:
        cp.wait_send()


COPIES = 73


def gather(q, k):
    rows, _, heads, hd = q.shape
    return pl.pallas_call(
        gather_kernel,
        out_shape=(
            jax.ShapeDtypeStruct((2, rows, heads, hd), q.dtype),
            jax.ShapeDtypeStruct((NZ, NX, 2, *k.shape[1:]), k.dtype),
        ),
        in_specs=[pl.BlockSpec(memory_space=pltpu.HBM), pl.BlockSpec(memory_space=pl.ANY)],
        out_specs=(pl.BlockSpec(memory_space=pltpu.HBM),) * 2,
        scratch_shapes=[
            pltpu.SemaphoreType.DMA((2,)),
            pltpu.SemaphoreType.DMA((COPIES,)),
            pltpu.SemaphoreType.DMA((COPIES,)),
        ],
        compiler_params=pltpu.CompilerParams(collective_id=0, has_side_effects=True),
        name="gather_keys",
    )(q, k)


def compute_kernel(
    pos_hbm, q_hbm, k_hbm, out_ref, q_ref, k_ref, e_ref, acc_ref, m_ref, w_ref, z_ref, seen_ref, pos_ref, sems, *, heads
):
    _, z, x, c = place()
    all_rows = w_ref.shape[0]
    rows = all_rows // heads
    width = k_ref.shape[2]
    tiles = width // 128
    parts = all_rows // QB
    chunks = k_ref.shape[0] // STEP

    def fetch(step):
        r = pl.ds(step * STEP, STEP)
        return pltpu.make_async_copy(k_hbm.at[r], k_ref.at[r], sems.at[2 + step])

    fetch_pos = pltpu.make_async_copy(pos_hbm, pos_ref, sems.at[0])
    fetch_pos.start()
    fetch_q = pltpu.make_async_copy(q_hbm, q_ref, sems.at[1])
    fetch_q.start()
    for step in range(chunks):
        fetch(step).start()
    acc_ref[...] = jnp.zeros_like(acc_ref)
    fetch_pos.wait()
    fetch_q.wait()
    fetch(0).wait()
    iota = lax.broadcasted_iota(jnp.int32, (QB, 128), 1)

    def block(i, carry):
        plane = jnp.where(i < BLOCKS // 2, z, NZ - 1 - z)
        r0 = (((plane * NX + x) * 2 + c) * (BLOCKS // 2) + lax.rem(i, BLOCKS // 2)) * rows
        lo, hi = pos_ref[r0], pos_ref[r0 + rows - 1]
        open_end = (lo + 1) // (STEP * width)
        start_masked = open_end * (STEP // MASKED)
        end = hi // (MASKED * width) + 1
        for t in range(rows):
            seen_ref[t * heads : (t + 1) * heads] = jnp.full((heads, 128), pos_ref[r0 + t], jnp.int32)

        def queries(u):
            return q_ref[pl.ds(pl.multiple_of(i * all_rows + u * QB, QB), QB), :]

        for u in range(parts):
            r = slice(u * QB, (u + 1) * QB)
            first = jnp.dot(queries(u), k_ref[0, :, 0:128], preferred_element_type=jnp.float32)
            first = jnp.max(jnp.where(iota <= seen_ref[r], first, NEG), axis=1, keepdims=True)
            m_ref[r] = jnp.broadcast_to(first * SCALE2, (QB, 128))
        z_ref[...] = jnp.zeros_like(z_ref)

        def sweep(count, masked):
            def body(step, carry):
                if not masked:

                    @pl.when((i == 0) & (step > 0))
                    def _():
                        fetch(step).wait()

                for u in range(parts):
                    r = slice(u * QB, (u + 1) * QB)
                    qb = queries(u)
                    total = None
                    for g in range(count):
                        b = step * count + g
                        s = jnp.dot(qb, k_ref[b], preferred_element_type=jnp.float32)
                        for l in range(tiles):
                            e = jnp.exp2(s[:, l * 128 : (l + 1) * 128] * SCALE2 - m_ref[r])
                            if masked:
                                e = jnp.where(iota + (b * width + l * 128) <= seen_ref[r], e, 0.0)
                            e_ref[b * tiles + l, r] = e
                            total = e if total is None else total + e
                    z_ref[r] += total
                return carry

            return body

        lax.fori_loop(0, open_end, sweep(STEP, False), 0)

        @pl.when(i == 0)
        def _():
            def rest(step, carry):
                fetch(step).wait()
                return carry

            lax.fori_loop(jnp.maximum(open_end, 1), chunks, rest, 0)

        lax.fori_loop(start_masked, end, sweep(MASKED, True), 0)

        def weigh():
            total = jnp.sum(z_ref[...], axis=1, keepdims=True)
            w_ref[...] = jnp.broadcast_to(1.0 / total, w_ref.shape)
            return total

        total = weigh()

        @pl.when(jnp.logical_not(jnp.max(total) <= BIG))
        def _():
            for u in range(parts):
                r = slice(u * QB, (u + 1) * QB)
                qb = queries(u)

                def largest(b, best):
                    s = jnp.dot(qb, k_ref[b], preferred_element_type=jnp.float32)
                    for l in range(tiles):
                        seen = iota + (b * width + l * 128) <= seen_ref[r]
                        best = jnp.maximum(best, jnp.where(seen, s[:, l * 128 : (l + 1) * 128], NEG))
                    return best

                best = lax.fori_loop(0, end * MASKED, largest, jnp.full((QB, 128), NEG, jnp.float32))
                m_ref[r] = jnp.broadcast_to(jnp.max(best, axis=1, keepdims=True) * SCALE2, (QB, 128))
            z_ref[...] = jnp.zeros_like(z_ref)
            lax.fori_loop(0, end * MASKED, sweep(1, True), 0)
            weigh()

        def columns(step, carry):
            for g in range(0, MASKED * tiles, 4):
                b = step * (MASKED * tiles) + g
                sums = [acc_ref[b + l] for l in range(4)]
                for t in range(all_rows // 8):
                    weight = w_ref[8 * t : 8 * t + 8]
                    for l in range(4):
                        sums[l] = sums[l] + e_ref[b + l, 8 * t : 8 * t + 8, :] * weight
                for l in range(4):
                    acc_ref[b + l] = sums[l]
            return carry

        lax.fori_loop(0, end, columns, 0)
        return carry

    lax.fori_loop(0, BLOCKS, block, 0)
    for zz in range(8):
        for cc in range(2):
            for l in range(tiles):
                out_ref[zz, cc, :, l * 128 : (l + 1) * 128] = jnp.concatenate(
                    [
                        jnp.sum(acc_ref[((zz * NX + xx) * 2 + cc) * tiles + l], axis=0, keepdims=True)
                        for xx in range(NX)
                    ],
                    0,
                )


def compute(places, q, k, heads):
    blocks, _, width = k.shape
    rows = q.shape[0] // BLOCKS
    row = pltpu.VMEM((rows, 128), jnp.float32)
    return pl.pallas_call(
        functools.partial(compute_kernel, heads=heads),
        out_shape=jax.ShapeDtypeStruct((8, 2, NX, width), jnp.float32),
        in_specs=[pl.BlockSpec(memory_space=pltpu.HBM)] * 3,
        out_specs=pl.BlockSpec(memory_space=pltpu.VMEM),
        scratch_shapes=[
            pltpu.VMEM(q.shape, q.dtype),
            pltpu.VMEM(k.shape, k.dtype),
            pltpu.VMEM((blocks * width // 128, rows, 128), jnp.float32),
            pltpu.VMEM((blocks * width // 128, 8, 128), jnp.float32),
            row,
            row,
            row,
            pltpu.VMEM((rows, 128), jnp.int32),
            pltpu.SMEM(places.shape, jnp.int32),
            pltpu.SemaphoreType.DMA((2 + blocks // STEP,)),
        ],
        compiler_params=pltpu.CompilerParams(vmem_limit_bytes=60 << 20),
        name="key_scores",
    )(places, q, k)


def reduce_kernel(p_ref, out_ref, own, b1, b2, rows, lsem, ssem, rsem, *, factor):
    y, z, x, c = place()

    def dev(yy, zz, xx, cc):
        return (yy, (zz * NX + xx) * 2 + cc)

    def turn(i, d, n):
        return lax.rem(i + d, n)

    first = [(turn(z, d, 8), turn(c, e, 2)) for e in range(2) for d in range(8) if d or e]
    second = [(turn(x, d, 4), turn(y, e, 4)) for e in range(4) for d in range(4) if d or e]
    barrier = pltpu.get_barrier_semaphore()
    for zz, cc in first:
        pl.semaphore_signal(barrier, inc=1, device_id=dev(y, zz, x, cc), device_id_type=MESH)
    for xx, yy in second:
        pl.semaphore_signal(barrier, inc=1, device_id=dev(yy, z, xx, c), device_id_type=MESH)
    keep = pltpu.make_async_copy(p_ref.at[z, c], own, lsem)
    keep.start()
    pl.semaphore_wait(barrier, 30)
    cps = []

    def send(src, dst, to):
        i = len(cps)
        cp = pltpu.make_async_remote_copy(
            src_ref=src, dst_ref=dst, send_sem=ssem.at[i], recv_sem=rsem.at[i], device_id=to, device_id_type=MESH
        )
        cp.start()
        cps.append(cp)

    for i, (zz, cc) in enumerate(first):
        send(p_ref.at[zz, cc], b1.at[i], dev(y, zz, x, cc))
    keep.wait()
    total = own[...]
    for i in range(15):
        cps[i].wait_recv()
        total = total + b1[i]
    for r in range(4):
        rows[r] = total[r : r + 1]
    for i, (xx, yy) in enumerate(second):
        send(rows.at[xx], b2.at[i], dev(yy, z, xx, c))
    total = rows[x]
    for i in range(15):
        cps[15 + i].wait_recv()
        total = total + b2[i]
    out_ref[...] = total * factor
    for cp in cps:
        cp.wait_send()


def reduce(partial, factor):
    tile = partial.shape[2:]
    return pl.pallas_call(
        functools.partial(reduce_kernel, factor=factor),
        out_shape=jax.ShapeDtypeStruct((1, tile[1]), jnp.float32),
        in_specs=[pl.BlockSpec(memory_space=pl.ANY)],
        out_specs=pl.BlockSpec(memory_space=pltpu.VMEM),
        scratch_shapes=[
            pltpu.VMEM(tile, jnp.float32),
            pltpu.VMEM((15, *tile), jnp.float32),
            pltpu.VMEM((15, 1, tile[1]), jnp.float32),
            pltpu.VMEM((4, 1, tile[1]), jnp.float32),
            pltpu.SemaphoreType.DMA,
            pltpu.SemaphoreType.DMA((30,)),
            pltpu.SemaphoreType.DMA((30,)),
        ],
        compiler_params=pltpu.CompilerParams(collective_id=1, has_side_effects=True),
        name="sum_scores",
    )(partial)


def on_device(sampled_rows, query_vectors, key_vectors):
    rows, all_heads, hd = query_vectors.shape
    groups = key_vectors.shape[1]
    heads = all_heads // groups
    q, k = gather(query_vectors.reshape(rows, groups, heads, hd), key_vectors.transpose(1, 2, 0))
    partial = compute(sampled_rows, q.reshape(-1, hd), k.reshape(-1, *k.shape[3:]), heads)
    return reduce(partial, 1.0 / heads).reshape(-1)


def solution(mesh):
    placed = (P(), P("seq", "kv", None), P("seq", "kv", None))
    return jax.shard_map(on_device, mesh=mesh, in_specs=placed, out_specs=P("seq"), check_vma=False)
```

time: 131 us -> 145 us (1.11)
  Pallas kernels: 126 us -> 142 us
  local copies, waits for them, and re-layouts: 4.57 us -> 2.89 us
    pallas_call x1, Pallas kernels: 26.7 us -> 34 us  [reduce(): pl.pallas_call(functools.partial(reduce_kernel, factor=factor), out_shape...]
    pallas_call x1, Pallas kernels: 65.3 us -> 71.8 us  [compute(): pl.pallas_call(functools.partial(compute_kernel, heads=heads), out_shape=...]
    pallas_call x1, Pallas kernels: 34.2 us -> 35.9 us  [gather(): pl.pallas_call(gather_kernel, out_shape=(jax.ShapeDtypeStruct((2, rows, h...]
    unnamed x8 -> x2, local copies, waits for them, and re-layouts: 4.57 us -> 2.89 us
where the time goes in v3:
time: 145 us
  Pallas kernels  142 us (98%)
  local copies, waits for them, and re-layouts  2.89 us (2%)
    pallas_call x1, Pallas kernels, compute(): pl.pallas_call(functools.partial(compute_kernel, heads=heads), out_shape=...  71.8 us
    pallas_call x1, Pallas kernels, gather(): pl.pallas_call(gather_kernel, out_shape=(jax.ShapeDtypeStruct((2, rows, h...  35.9 us
    pallas_call x1, Pallas kernels, reduce(): pl.pallas_call(functools.partial(reduce_kernel, factor=factor), out_shape...  34 us

profile of v3, /device:TPU:1, one launch (start us, length us, event | category | flops | bytes accessed | tf_op | source)
XLA Modules:
  0.0 144.6 jit_solution(1347624466566186583)
XLA Ops:
  0.0 1.7 %copy.4 = bf16[256,2,128]{0,2,1:T(8,128)(2,1)} copy(bf16[256,2,128]{2,1,0:T(2,128)(2,1)} %param.5) | data formatting | bytes 262144 | tf_op args[2]
  1.7 35.9 %gather_keys.1 = (bf16[2,96,8,128]{3,2,1,0:T(8,128)(2,1)}, bf16[8,4,2,128,256]{4,3,2,1,0:T(8,128)(2,1)}) custom-call(bf16[96,2,8,128]{3,2,1,0:T(8,128)(2,1)} %bitcast.8, bf16[2,128,256]{2,1,0:T(8,128)(2,1)} %bitcast.6), custom_call_target="tpu_custom_call" | custom-call | tf_op jit(solution)/shard_map/gather_keys/pallas_call | solution.py:154
  37.5 71.8 %key_scores.1.p_ref = f32[8,2,4,256]{3,2,1,0:T(4,128)} custom-call(s32[6144]{0:T(1024)} %pos_hbm.1, bf16[1536,128]{1,0:T(8,128)(2,1)} %bitcast.7, bf16[64,128,256]{2,1,0:T(8,128)(2,1)} %bitcast.5), custom_call_target="tpu_custom_call" | custom-call | tf_op jit(solution)/shard_map/key_scores/pallas_call | solution.py:315
  109.3 34.0 %sum_scores.1 = f32[1,256]{1,0:T(1,128)} custom-call(f32[8,2,4,256]{3,2,1,0:T(4,128)} %key_scores.1.p_ref), custom_call_target="tpu_custom_call" | custom-call | tf_op jit(solution)/shard_map/sum_scores/pallas_call | solution.py:388
  143.4 1.2 copy.6

commit v4 on v3

--- a/solution.py
+++ b/solution.py
@@ -26,7 +26,9 @@
     return lax.axis_index("kv"), seq // 8, lax.rem(seq // 2, 4), lax.rem(seq, 2)
 
 
-def gather_kernel(q_ref, k_ref, qo_ref, ko_ref, lsem, ssem, rsem):
+DOUBLE = (4,)
+
+def gather_kernel(q_ref, k_ref, qo_ref, ko_ref, held, lsem, ssem, rsem):
     y, z, x, c = place()
     head = lax.rem(z, 2)
     half = k_ref.shape[1] // 2
@@ -41,14 +43,14 @@
         return lax.rem(x + d + NX, NX)
 
     partner = dev(z, x, 1 - c)
-    mirror = dev(NZ - 1 - z, x, c)
+    mirror = dev(NZ - 1 - z, x, 1 - c)
     barrier = pltpu.get_barrier_semaphore()
     peers = [partner, mirror]
-    peers += [dev(zn(d), x, c) for d in (1, -1, 2, -2, 3, -3)]
-    peers += [dev(z, xn(d), c) for d in DIRS]
+    peers += [dev(zn(d), x, c) for d in (1, -1, 2, -2)]
+    peers += [dev(z, xn(d), cc) for d in DIRS for cc in (c, 1 - c)]
     for p in peers:
         pl.semaphore_signal(barrier, inc=1, device_id=p, device_id_type=MESH)
-    local_k = pltpu.make_async_copy(k_ref.at[head], ko_ref.at[z, x, c], lsem.at[0])
+    local_k = pltpu.make_async_copy(k_ref.at[head], held.at[z, x, c], lsem.at[0])
     local_k.start()
     local_q = pltpu.make_async_copy(q_ref.at[:, head], qo_ref.at[0], lsem.at[1])
     local_q.start()
@@ -66,7 +68,7 @@
         return cp
 
     def block(zz, xx, piece=None):
-        ref = ko_ref.at[zz, xx, c]
+        ref = held.at[zz, xx, c]
         return ref if piece is None else ref.at[pl.ds(piece * half, half)]
 
     def move(zz, xx, to, piece=None):
@@ -81,16 +83,27 @@
         ax[(0, d)] = send(k_ref.at[head], mine, dev(z, xn(d), c))
     for d in DIRS:
         az[2 * d] = send(k_ref.at[head], mine, dev(zn(2 * d), x, c))
-    for d in DIRS:
-        az[3 * d] = send(k_ref.at[1 - head], mine, dev(zn(3 * d), x, c))
-    twin = [send(k_ref.at[head], mine, partner)]
+    twin = {zd: [] for zd in range(-3, 5)}
+    twin[0].append(send(k_ref.at[head], mine, partner))
     fx = {}
+    outs = []
+
+    def write(zd, cc):
+        zz = zn(zd)
+        cp = pltpu.make_async_copy(held.at[zz, :, cc], ko_ref.at[zz, :, cc], lsem.at[2 + len(outs)])
+        cp.start()
+        outs.append(cp)
+
+    def write_twin(zd):
+        for cp in twin[zd]:
+            cp.wait_recv()
+        write(zd, 1 - c)
 
     def spread(zd):
         zz = zn(zd)
         for d in DIRS:
             ax[(zd, d)] = move(zz, x, dev(z, xn(d), c))
-        twin.append(move(zz, x, partner))
+        twin[zd].append(move(zz, x, partner))
 
     def forward(zd):
         zz = zn(zd)
@@ -98,29 +111,36 @@
             ax[(zd, d)].wait_recv()
         for d in DIRS:
             fx[(zd, d)] = move(zz, xn(-d), dev(z, xn(d), c), 0 if d == 1 else 1)
+        if zd in DOUBLE:
+            for d in DIRS:
+                twin[zd].append(move(zz, xn(-d), dev(z, xn(d), 1 - c), 0 if d == 1 else 1))
         for d in DIRS:
-            twin.append(move(zz, xn(-d), partner))
+            twin[zd].append(move(zz, xn(-d), partner))
 
     def finish(zd):
         for d in DIRS:
             fx[(zd, d)].wait_recv()
-        twin.append(move(zn(zd), xn(2), partner))
-
-    for d in DIRS:
-        az[-d].wait_recv()
-        spread(d)
+        if zd not in DOUBLE:
+            twin[zd].append(move(zn(zd), xn(2), partner))
+        write(zd, c)
+
+    for d in DIRS:
+        az[d].wait_recv()
+        az[3 * d] = move(zn(-d), x, dev(zn(2 * d), x, c))
+        spread(-d)
     forward(0)
     for d in DIRS:
         az[-2 * d].wait_recv()
     far = {d: move(zn(2 * d), x, dev(zn(-2 * d), x, c), 0 if d == 1 else 1) for d in DIRS}
     for d in DIRS:
         spread(2 * d)
-    swap = send(q_ref.at[:, 1 - head], qo_ref.at[1], mirror)
     for d in DIRS:
         forward(d)
     for d in DIRS:
         az[-3 * d].wait_recv()
         spread(3 * d)
+    swap = send(q_ref.at[:, 1 - head], qo_ref.at[1], mirror)
+    local_k.wait()
     finish(0)
     for d in DIRS:
         forward(2 * d)
@@ -136,17 +156,20 @@
     forward(4)
     for d in DIRS:
         finish(3 * d)
+    for zd in (0, 1, -1, 2, -2):
+        write_twin(zd)
     finish(4)
-    local_k.wait()
+    for zd in (3, -3, 4):
+        write_twin(zd)
     local_q.wait()
     swap.wait_recv()
-    for cp in twin:
-        cp.wait_recv()
+    for cp in outs:
+        cp.wait()
     for cp in sends:
         cp.wait_send()
 
 
-COPIES = 73
+COPIES = 74
 
 
 def gather(q, k):
@@ -160,11 +183,12 @@
         in_specs=[pl.BlockSpec(memory_space=pltpu.HBM), pl.BlockSpec(memory_space=pl.ANY)],
         out_specs=(pl.BlockSpec(memory_space=pltpu.HBM),) * 2,
         scratch_shapes=[
-            pltpu.SemaphoreType.DMA((2,)),
+            pltpu.VMEM((NZ, NX, 2, *k.shape[1:]), k.dtype),
+            pltpu.SemaphoreType.DMA((2 + 2 * NZ,)),
             pltpu.SemaphoreType.DMA((COPIES,)),
             pltpu.SemaphoreType.DMA((COPIES,)),
         ],
-        compiler_params=pltpu.CompilerParams(collective_id=0, has_side_effects=True),
+        compiler_params=pltpu.CompilerParams(collective_id=0, has_side_effects=True, vmem_limit_bytes=60 << 20),
         name="gather_keys",
     )(q, k)
 
@@ -198,7 +222,8 @@
 
     def block(i, carry):
         plane = jnp.where(i < BLOCKS // 2, z, NZ - 1 - z)
-        r0 = (((plane * NX + x) * 2 + c) * (BLOCKS // 2) + lax.rem(i, BLOCKS // 2)) * rows
+        core = jnp.where(i < BLOCKS // 2, c, 1 - c)
+        r0 = (((plane * NX + x) * 2 + core) * (BLOCKS // 2) + lax.rem(i, BLOCKS // 2)) * rows
         lo, hi = pos_ref[r0], pos_ref[r0 + rows - 1]
         open_end = (lo + 1) // (STEP * width)
         start_masked = open_end * (STEP // MASKED)
@@ -334,7 +359,7 @@
     )(places, q, k)
 
 
-def reduce_kernel(p_ref, out_ref, own, b1, b2, rows, lsem, ssem, rsem, *, factor):
+def reduce_kernel(p_ref, out_ref, own, b1, b2, rows, lsem, ssem, rsem):
     y, z, x, c = place()
 
     def dev(yy, zz, xx, cc):
@@ -378,15 +403,15 @@
     for i in range(15):
         cps[15 + i].wait_recv()
         total = total + b2[i]
-    out_ref[...] = total * factor
+    out_ref[...] = total
     for cp in cps:
         cp.wait_send()
 
 
-def reduce(partial, factor):
+def reduce(partial):
     tile = partial.shape[2:]
     return pl.pallas_call(
-        functools.partial(reduce_kernel, factor=factor),
+        reduce_kernel,
         out_shape=jax.ShapeDtypeStruct((1, tile[1]), jnp.float32),
         in_specs=[pl.BlockSpec(memory_space=pl.ANY)],
         out_specs=pl.BlockSpec(memory_space=pltpu.VMEM),
@@ -410,7 +435,7 @@
     heads = all_heads // groups
     q, k = gather(query_vectors.reshape(rows, groups, heads, hd), key_vectors.transpose(1, 2, 0))
     partial = compute(sampled_rows, q.reshape(-1, hd), k.reshape(-1, *k.shape[3:]), heads)
-    return reduce(partial, 1.0 / heads).reshape(-1)
+    return reduce(partial).reshape(-1) * (1.0 / heads)
 
 
 def solution(mesh):

time: 145 us -> 137 us (0.945)
  Pallas kernels: 142 us -> 134 us
    pallas_call x1, Pallas kernels: 34 us -> 27.7 us  [reduce(): pl.pallas_call(reduce_kernel, out_shape=jax.ShapeDtypeStruct((1, tile[1])...]
where the time goes in v4:
time: 137 us
  Pallas kernels  134 us (98%)
  local copies, waits for them, and re-layouts  1.67 us (1%)
    pallas_call x1, Pallas kernels, compute(): pl.pallas_call(functools.partial(compute_kernel, heads=heads), out_shape=...  71.8 us
    pallas_call x1, Pallas kernels, gather(): pl.pallas_call(gather_kernel, out_shape=(jax.ShapeDtypeStruct((2, rows, h...  34.5 us
    pallas_call x1, Pallas kernels, reduce(): pl.pallas_call(reduce_kernel, out_shape=jax.ShapeDtypeStruct((1, tile[1])...  27.7 us

profile of v4, /device:TPU:1, one launch (start us, length us, event | category | flops | bytes accessed | tf_op | source)
XLA Modules:
  0.0 137.0 jit_solution(1939735565296398092)
XLA Ops:
  0.0 1.7 %copy.4 = bf16[256,2,128]{0,2,1:T(8,128)(2,1)} copy(bf16[256,2,128]{2,1,0:T(2,128)(2,1)} %param.5) | data formatting | bytes 262144 | tf_op args[2]
  1.7 34.5 %gather_keys.1 = (bf16[2,96,8,128]{3,2,1,0:T(8,128)(2,1)}, bf16[8,4,2,128,256]{4,3,2,1,0:T(8,128)(2,1)}) custom-call(bf16[96,2,8,128]{3,2,1,0:T(8,128)(2,1)} %bitcast.8, bf16[2,128,256]{2,1,0:T(8,128)(2,1)} %bitcast.6), custom_call_target="tpu_custom_call" | custom-call | tf_op jit(solution)/shard_map/gather_keys/pallas_call | solution.py:177
  36.2 71.8 %key_scores.1.p_ref = f32[8,2,4,256]{3,2,1,0:T(4,128)} custom-call(s32[6144]{0:T(1024)} %pos_hbm.1, bf16[1536,128]{1,0:T(8,128)(2,1)} %bitcast.7, bf16[64,128,256]{2,1,0:T(8,128)(2,1)} %bitcast.5), custom_call_target="tpu_custom_call" | custom-call | tf_op jit(solution)/shard_map/key_scores/pallas_call | solution.py:340
  108.0 27.7 %sum_scores.1 = f32[1,256]{1,0:T(1,128)} custom-call(f32[8,2,4,256]{3,2,1,0:T(4,128)} %key_scores.1.p_ref), custom_call_target="tpu_custom_call" | custom-call | tf_op jit(solution)/shard_map/sum_scores/pallas_call | solution.py:413
  135.7 1.2 broadcast_multiply_fusion

commit v5 on v4

--- a/solution.py
+++ b/solution.py
@@ -28,8 +28,10 @@
 
 DOUBLE = (4,)
 
-def gather_kernel(q_ref, k_ref, qo_ref, ko_ref, held, lsem, ssem, rsem):
+def gather_kernel(q_ref, raw_hbm, qo_ref, ko_ref, held, raw, k_ref, lsem, ssem, rsem):
     y, z, x, c = place()
+    fetch = pltpu.make_async_copy(raw_hbm, raw, lsem.at[2 + 2 * NZ])
+    fetch.start()
     head = lax.rem(z, 2)
     half = k_ref.shape[1] // 2
 
@@ -50,6 +52,9 @@
     peers += [dev(z, xn(d), cc) for d in DIRS for cc in (c, 1 - c)]
     for p in peers:
         pl.semaphore_signal(barrier, inc=1, device_id=p, device_id_type=MESH)
+    fetch.wait()
+    for h in range(k_ref.shape[0]):
+        k_ref[h] = jnp.transpose(raw[:, h, :])
     local_k = pltpu.make_async_copy(k_ref.at[head], held.at[z, x, c], lsem.at[0])
     local_k.start()
     local_q = pltpu.make_async_copy(q_ref.at[:, head], qo_ref.at[0], lsem.at[1])
@@ -178,13 +183,15 @@
         gather_kernel,
         out_shape=(
             jax.ShapeDtypeStruct((2, rows, heads, hd), q.dtype),
-            jax.ShapeDtypeStruct((NZ, NX, 2, *k.shape[1:]), k.dtype),
+            jax.ShapeDtypeStruct((NZ, NX, 2, k.shape[2], k.shape[0]), k.dtype),
         ),
         in_specs=[pl.BlockSpec(memory_space=pltpu.HBM), pl.BlockSpec(memory_space=pl.ANY)],
         out_specs=(pl.BlockSpec(memory_space=pltpu.HBM),) * 2,
         scratch_shapes=[
-            pltpu.VMEM((NZ, NX, 2, *k.shape[1:]), k.dtype),
-            pltpu.SemaphoreType.DMA((2 + 2 * NZ,)),
+            pltpu.VMEM((NZ, NX, 2, k.shape[2], k.shape[0]), k.dtype),
+            pltpu.VMEM(k.shape, k.dtype),
+            pltpu.VMEM((k.shape[1], k.shape[2], k.shape[0]), k.dtype),
+            pltpu.SemaphoreType.DMA((3 + 2 * NZ,)),
             pltpu.SemaphoreType.DMA((COPIES,)),
             pltpu.SemaphoreType.DMA((COPIES,)),
         ],
@@ -368,8 +375,15 @@
     def turn(i, d, n):
         return lax.rem(i + d, n)
 
-    first = [(turn(z, d, 8), turn(c, e, 2)) for e in range(2) for d in range(8) if d or e]
-    second = [(turn(x, d, 4), turn(y, e, 4)) for e in range(4) for d in range(4) if d or e]
+    def hops(d, n):
+        return min(d, n - d)
+
+    steps = sorted(((d, e) for d in range(8) for e in range(2) if d or e), key=lambda s: -hops(s[0], 8) - s[1])
+    first = [(turn(z, d, 8), turn(c, e, 2)) for d, e in steps]
+    steps = sorted(
+        ((d, e) for d in range(4) for e in range(4) if d or e), key=lambda s: -hops(s[0], 4) - hops(s[1], 4)
+    )
+    second = [(turn(x, d, 4), turn(y, e, 4)) for d, e in steps]
     barrier = pltpu.get_barrier_semaphore()
     for zz, cc in first:
         pl.semaphore_signal(barrier, inc=1, device_id=dev(y, zz, x, cc), device_id_type=MESH)
@@ -433,7 +447,7 @@
     rows, all_heads, hd = query_vectors.shape
     groups = key_vectors.shape[1]
     heads = all_heads // groups
-    q, k = gather(query_vectors.reshape(rows, groups, heads, hd), key_vectors.transpose(1, 2, 0))
+    q, k = gather(query_vectors.reshape(rows, groups, heads, hd), key_vectors)
     partial = compute(sampled_rows, q.reshape(-1, hd), k.reshape(-1, *k.shape[3:]), heads)
     return reduce(partial).reshape(-1) * (1.0 / heads)
 

time: 137 us -> 135 us (0.985)
  local copies, waits for them, and re-layouts: 1.67 us -> 0 us
    unnamed x1 -> x0, local copies, waits for them, and re-layouts: 1.67 us -> none
where the time goes in v5:
time: 135 us
  Pallas kernels  134 us (99%)
    pallas_call x1, Pallas kernels, compute(): pl.pallas_call(functools.partial(compute_kernel, heads=heads), out_shape=...  71.8 us
    pallas_call x1, Pallas kernels, gather(): pl.pallas_call(gather_kernel, out_shape=(jax.ShapeDtypeStruct((2, rows, h...  34.2 us
    pallas_call x1, Pallas kernels, reduce(): pl.pallas_call(reduce_kernel, out_shape=jax.ShapeDtypeStruct((1, tile[1])...  27.7 us

profile of v5, /device:TPU:1, one launch (start us, length us, event | category | flops | bytes accessed | tf_op | source)
XLA Modules:
  0.0 135.0 jit_solution(10676411609118401483)
XLA Ops:
  0.0 34.2 %gather_keys.1 = (bf16[2,96,8,128]{3,2,1,0:T(8,128)(2,1)}, bf16[8,4,2,128,256]{4,3,2,1,0:T(8,128)(2,1)}) custom-call(bf16[96,2,8,128]{3,2,1,0:T(8,128)(2,1)} %bitcast.6, bf16[256,2,128]{2,1,0:T(2,128)(2,1)} %raw_hbm.1), custom_call_target="tpu_custom_call" | custom-call | tf_op jit(solution)/shard_map/gather_keys/pallas_call | solution.py:182
  34.2 71.8 %key_scores.1.p_ref = f32[8,2,4,256]{3,2,1,0:T(4,128)} custom-call(s32[6144]{0:T(1024)} %pos_hbm.1, bf16[1536,128]{1,0:T(8,128)(2,1)} %bitcast.5, bf16[64,128,256]{2,1,0:T(8,128)(2,1)} %bitcast.4), custom_call_target="tpu_custom_call" | custom-call | tf_op jit(solution)/shard_map/key_scores/pallas_call | solution.py:347
  106.0 27.7 %sum_scores.1 = f32[1,256]{1,0:T(1,128)} custom-call(f32[8,2,4,256]{3,2,1,0:T(4,128)} %key_scores.1.p_ref), custom_call_target="tpu_custom_call" | custom-call | tf_op jit(solution)/shard_map/sum_scores/pallas_call | solution.py:427
  133.8 1.2 broadcast_multiply_fusion

commit v6 on v5

--- a/solution.py
+++ b/solution.py
@@ -438,7 +438,7 @@
             pltpu.SemaphoreType.DMA((30,)),
             pltpu.SemaphoreType.DMA((30,)),
         ],
-        compiler_params=pltpu.CompilerParams(collective_id=1, has_side_effects=True),
+        compiler_params=pltpu.CompilerParams(collective_id=1, has_side_effects=True, vmem_limit_bytes=431 << 17),
         name="sum_scores",
     )(partial)
 

time: 135 us -> 134 us (level)
  no operation moved by 1% of the time
where the time goes in v6:
time: 134 us
  Pallas kernels  133 us (99%)
    pallas_call x1, Pallas kernels, compute(): pl.pallas_call(functools.partial(compute_kernel, heads=heads), out_shape=...  72.4 us
    pallas_call x1, Pallas kernels, gather(): pl.pallas_call(gather_kernel, out_shape=(jax.ShapeDtypeStruct((2, rows, h...  34.2 us
    pallas_call x1, Pallas kernels, reduce(): pl.pallas_call(reduce_kernel, out_shape=jax.ShapeDtypeStruct((1, tile[1])...  26.6 us

profile of v6, /device:TPU:1, one launch (start us, length us, event | category | flops | bytes accessed | tf_op | source)
XLA Modules:
  0.0 133.8 jit_solution(14240047064911154814)
XLA Ops:
  0.0 34.2 %gather_keys.1 = (bf16[2,96,8,128]{3,2,1,0:T(8,128)(2,1)}, bf16[8,4,2,128,256]{4,3,2,1,0:T(8,128)(2,1)}) custom-call(bf16[96,2,8,128]{3,2,1,0:T(8,128)(2,1)} %bitcast.6, bf16[256,2,128]{2,1,0:T(2,128)(2,1)} %raw_hbm.1), custom_call_target="tpu_custom_call" | custom-call | tf_op jit(solution)/shard_map/gather_keys/pallas_call | solution.py:182
  34.2 72.4 %key_scores.1.p_ref = f32[8,2,4,256]{3,2,1,0:T(4,128)} custom-call(s32[6144]{0:T(1024)} %pos_hbm.1, bf16[1536,128]{1,0:T(8,128)(2,1)} %bitcast.5, bf16[64,128,256]{2,1,0:T(8,128)(2,1)} %bitcast.4), custom_call_target="tpu_custom_call" | custom-call | tf_op jit(solution)/shard_map/key_scores/pallas_call | solution.py:347
  106.7 26.6 %sum_scores.1 = f32[1,256]{1,0:T(1,128)S(1)} custom-call(f32[8,2,4,256]{3,2,1,0:T(4,128)} %key_scores.1.p_ref), custom_call_target="tpu_custom_call" | custom-call | tf_op jit(solution)/shard_map/sum_scores/pallas_call | solution.py:427
  133.3 0.6 broadcast_multiply_fusion

commit v7 on v6

--- a/solution.py
+++ b/solution.py
@@ -228,8 +228,11 @@
     iota = lax.broadcasted_iota(jnp.int32, (QB, 128), 1)
 
     def block(i, carry):
-        plane = jnp.where(i < BLOCKS // 2, z, NZ - 1 - z)
-        core = jnp.where(i < BLOCKS // 2, c, 1 - c)
+        late = jnp.maximum(z, NZ - 1 - z)
+        plane = jnp.where(i < BLOCKS // 2, late, NZ - 1 - late)
+        own = plane == z
+        core = jnp.where(own, c, 1 - c)
+        slot = jnp.where(own, 0, BLOCKS // 2) + lax.rem(i, BLOCKS // 2)
         r0 = (((plane * NX + x) * 2 + core) * (BLOCKS // 2) + lax.rem(i, BLOCKS // 2)) * rows
         lo, hi = pos_ref[r0], pos_ref[r0 + rows - 1]
         open_end = (lo + 1) // (STEP * width)
@@ -239,7 +242,7 @@
             seen_ref[t * heads : (t + 1) * heads] = jnp.full((heads, 128), pos_ref[r0 + t], jnp.int32)
 
         def queries(u):
-            return q_ref[pl.ds(pl.multiple_of(i * all_rows + u * QB, QB), QB), :]
+            return q_ref[pl.ds(pl.multiple_of(slot * all_rows + u * QB, QB), QB), :]
 
         for u in range(parts):
             r = slice(u * QB, (u + 1) * QB)

time: 134 us -> 134 us (level)
    pallas_call x1, Pallas kernels: 72.4 us -> 71 us  [compute(): pl.pallas_call(functools.partial(compute_kernel, heads=heads), out_shape=...]
    pallas_call x1, Pallas kernels: 26.6 us -> 28 us  [reduce(): pl.pallas_call(reduce_kernel, out_shape=jax.ShapeDtypeStruct((1, tile[1])...]
where the time goes in v7:
time: 134 us
  Pallas kernels  133 us (99%)
    pallas_call x1, Pallas kernels, compute(): pl.pallas_call(functools.partial(compute_kernel, heads=heads), out_shape=...  71 us
    pallas_call x1, Pallas kernels, gather(): pl.pallas_call(gather_kernel, out_shape=(jax.ShapeDtypeStruct((2, rows, h...  34.2 us
    pallas_call x1, Pallas kernels, reduce(): pl.pallas_call(reduce_kernel, out_shape=jax.ShapeDtypeStruct((1, tile[1])...  28 us

profile of v7, /device:TPU:1, one launch (start us, length us, event | category | flops | bytes accessed | tf_op | source)
XLA Modules:
  0.0 133.8 jit_solution(3356548728384067639)
XLA Ops:
  0.0 34.2 %gather_keys.1 = (bf16[2,96,8,128]{3,2,1,0:T(8,128)(2,1)}, bf16[8,4,2,128,256]{4,3,2,1,0:T(8,128)(2,1)}) custom-call(bf16[96,2,8,128]{3,2,1,0:T(8,128)(2,1)} %bitcast.6, bf16[256,2,128]{2,1,0:T(2,128)(2,1)} %raw_hbm.1), custom_call_target="tpu_custom_call" | custom-call | tf_op jit(solution)/shard_map/gather_keys/pallas_call | solution.py:182
  34.2 71.0 %key_scores.1.p_ref = f32[8,2,4,256]{3,2,1,0:T(4,128)} custom-call(s32[6144]{0:T(1024)} %pos_hbm.1, bf16[1536,128]{1,0:T(8,128)(2,1)} %bitcast.5, bf16[64,128,256]{2,1,0:T(8,128)(2,1)} %bitcast.4), custom_call_target="tpu_custom_call" | custom-call | tf_op jit(solution)/shard_map/key_scores/pallas_call | solution.py:350
  105.3 28.0 %sum_scores.1 = f32[1,256]{1,0:T(1,128)S(1)} custom-call(f32[8,2,4,256]{3,2,1,0:T(4,128)} %key_scores.1.p_ref), custom_call_target="tpu_custom_call" | custom-call | tf_op jit(solution)/shard_map/sum_scores/pallas_call | solution.py:430
  133.2 0.6 broadcast_multiply_fusion
